TPU v7x, 128 devices: a whole 4x4x4 slice. The times are simulated.
128 devices in a mesh: lat: 8 (over z, y_hi), lon: 16 (over y_lo, x, core).
Axes of the slice: x: 4, y: 4 (y_hi: 2, y_lo: 2; y = y_hi * 2 + y_lo), z: 4, core: 2. Of those that a mesh axis runs over, the one named last changes fastest.
Arguments:
- mesh_nodes: bfloat16 [65536, 512], P(('lat', 'lon')), may hold values from -6 to 6
- norm_gain: float32 [512], replicated, may hold values from 0.5 to 1.5
- w_query: bfloat16 [512, 512], replicated, may hold values from -0.25 to 0.25
- w_node_kv: bfloat16 [512, 1024], replicated, may hold values from -0.25 to 0.25
- obs_rows: bfloat16 [65536, 256], P(('lat', 'lon')), may hold values from -82 to 82
- w_obs_kv: bfloat16 [256, 1024], replicated, may hold values from -0.375 to 0.375
- obs_owner: int32 [65536, 1], P(('lat', 'lon')), may hold values from 0 to 127; in each aligned block of 512 rows (0 to 511, 512 to 1023, ...) at most 8 rows name the same one
- neighbours: int32 [65536, 32], P(('lat', 'lon')), may hold values from 0 to 1023
- neighbour_mask: int32 [65536, 32], P(('lat', 'lon')), may hold values 0 or 1
- disk_tokens: bfloat16 [1024, 5, 256], P(('lat', 'lon')), may hold values from -6 to 6
- w_disk_kv: bfloat16 [256, 1024], replicated, may hold values from -0.375 to 0.375
- disk_start: int32 [5], replicated, may hold values from 0 to 15
- disk_extent: int32 [5], replicated, may hold values from 4 to 8
- w_out: bfloat16 [512, 512], replicated, may hold values from -0.25 to 0.25
Outputs:
- updated: bfloat16 [65536, 512], P(('lat', 'lon'))
Inputs may be any that keep to these rules, and one draw needn't show every extreme that they name: `obs_owner`: in the rows of one device, no owner is named more than 8 times, a bound that some block reaches.
All inputs are finite; a program needn't handle non-finite values. No bound on the sum of `neighbour_mask` on one device may be relied on, other than what follows from the above.
Results may differ from a plain program's by a relative error of at most 0.0039.
The roundings to bfloat16 on the way count: a program that leaves them out, or rounds other values in their place, can miss the bound.
Values may be sent and summed in bfloat16 or wider, within the bound.
No kernel may reach another device: no remote copies, remote signals or barrier semaphores. Data moves between devices by JAX's collectives and lax.ppermute only.
A program may use at most 128 MiB of HBM per device.

v0:
```python
import functools

import jax
import jax.numpy as jnp
from jax import lax
from jax.experimental import pallas as pl
from jax.experimental.pallas import tpu as pltpu
from jax.sharding import PartitionSpec as P

HEADS = 8
AXES = ("lat", "lon")
LOG2E = 1.4426950408889634
EMPTY = 65536.0
NEG = -1e30
BIG = 2.0**100
F32 = jnp.float32
BF16 = jnp.bfloat16
NT = (((1,), (1,)), ((), ()))


def shape(dims, dtype):
    return jax.ShapeDtypeStruct(dims, dtype)


def params(grant=60 * 1024 * 1024):
    return pltpu.CompilerParams(vmem_limit_bytes=grant)


HBM = pl.BlockSpec(memory_space=pltpu.HBM)
VMEM = pl.BlockSpec(memory_space=pltpu.VMEM)
SMEM = pl.BlockSpec(memory_space=pltpu.SMEM)


def start_copy(source, target, sem):
    copy = pltpu.make_async_copy(source, target, sem)
    copy.start()
    return copy


def place_kernel(owner_ref, rows_ref, send_ref, held_ref, sems):
    count = rows_ref.shape[0]
    slots = send_ref.shape[0]
    owners = slots // 8
    owner = owner_ref[...]
    hot = jnp.where(lax.broadcasted_iota(jnp.int32, (owners, count), 0) == owner, 1.0, 0.0)
    row = lax.broadcasted_iota(jnp.int32, (count, count), 0)
    col = lax.broadcasted_iota(jnp.int32, (count, count), 1)
    earlier = jnp.where(row < col, 1.0, 0.0).astype(BF16)
    before = jnp.dot(hot.astype(BF16), earlier, preferred_element_type=F32)
    rank = jnp.sum(before * hot, axis=0, keepdims=True)
    slot = owner * 8 + rank.astype(jnp.int32)
    rows = rows_ref[...]
    ones_rows = jnp.ones((count, 128), BF16)
    step = slots // 4
    copies = []
    for i in range(4):
        at = pl.ds(i * step, step)
        ids_col = lax.broadcasted_iota(jnp.int32, (step, count), 0) + i * step
        placing = jnp.where(ids_col == slot, 1.0, 0.0).astype(BF16)
        placed = jnp.dot(placing, rows, preferred_element_type=F32)
        filled = jnp.dot(placing, ones_rows, preferred_element_type=F32)
        filled = jnp.concatenate([filled, filled], axis=1)
        held_ref[at, :] = jnp.where(filled > 0.5, placed, EMPTY).astype(BF16)
        copies.append(start_copy(held_ref.at[at, :], send_ref.at[at, :], sems.at[i]))
    for copy in copies:
        copy.wait()


def place(owner, rows, slots):
    return pl.pallas_call(
        place_kernel,
        out_shape=shape((slots, rows.shape[1]), BF16),
        in_specs=[VMEM, VMEM],
        out_specs=HBM,
        scratch_shapes=[pltpu.VMEM((slots, rows.shape[1]), BF16), pltpu.SemaphoreType.DMA((4,))],
        compiler_params=params(67043328),
        cost_estimate=pl.CostEstimate(flops=10**9, bytes_accessed=10**6, transcendentals=0),
        name="place",
    )(owner, rows)


def one_head(pair, odd):
    lane = lax.broadcasted_iota(jnp.int32, pair.shape, 1)
    keep = lane >= 64 if odd else lane < 64
    return jnp.where(keep, pair.astype(F32), 0.0).astype(pair.dtype)


def prep_kernel(
    near_ref, mark_ref, x_hbm, gain_ref, wq_hbm, wkv_hbm, wd_hbm, all_hbm, own_hbm,
    x_ref, wq_ref, wkv_ref, wd_ref, all_ref, own_ref, list_ref, sems, out_sems,
):
    n, d = x_ref.shape
    slots = 1024
    get_x = start_copy(x_hbm, x_ref, sems.at[0])
    get_wq = start_copy(wq_hbm, wq_ref, sems.at[1])
    get_wkv = start_copy(wkv_hbm, wkv_ref, sems.at[2])
    get_wd = start_copy(wd_hbm, wd_ref, sems.at[3])
    list_ref[...] = jnp.transpose(jnp.where(mark_ref[...] > 0, near_ref[...], -1), (1, 0))
    step = 64

    def body(i, carry):
        start = pl.multiple_of(i * step, step)
        near = list_ref[pl.ds(start, step), :].astype(jnp.int16)
        ids = lax.broadcasted_iota(jnp.int16, (step, slots), 1)
        total = jnp.zeros((step, slots), jnp.int16)
        one = jnp.ones((step, slots), jnp.int16)
        for entry in range(near.shape[1]):
            total = jnp.where(ids == near[:, entry : entry + 1], total + one, total)
        count = total.astype(F32).astype(BF16)
        for j in range(4):
            at = pl.ds(pl.multiple_of((12 + j) * n + start, step), step)
            all_ref[at, :] = count[:, j * 256 : j * 256 + 256]
        return carry

    lax.fori_loop(0, n // step, body, 0)

    def put(block, blocks, sem):
        at = pl.ds(block * n, blocks * n)
        return start_copy(all_ref.at[at, :], all_hbm.at[at, :], out_sems.at[sem])

    puts = [put(12, 4, 0)]
    get_x.wait()
    x = x_ref[...].astype(F32)
    inverse = lax.rsqrt(jnp.mean(x * x, axis=1, keepdims=True) + 1e-06)
    normed = (x * inverse * gain_ref[...]).astype(BF16)
    get_wq.wait()
    query = (jnp.dot(normed, wq_ref[...], preferred_element_type=F32) * 0.125).astype(BF16)
    get_wkv.wait()
    kv = jnp.dot(normed, wkv_ref[...], preferred_element_type=F32).astype(BF16)
    for j in range(2):
        all_ref[pl.ds((8 + j) * n, n), :] = query[:, j * 256 : j * 256 + 256]
        all_ref[pl.ds((10 + j) * n, n), :] = kv[:, d + j * 256 : d + j * 256 + 256]
    puts.append(put(8, 4, 1))
    prod = query.astype(F32) * kv[:, :d].astype(F32)
    lane = lax.broadcasted_iota(jnp.int32, (n, 128), 1)
    own = jnp.zeros((n, 128), F32)
    get_wd.wait()
    for head in range(HEADS):
        lo = head // 2 * 128
        part = jnp.sum(prod[:, head * 64 : head * 64 + 64], axis=1, keepdims=True) * LOG2E
        own = jnp.where(lane == head, part, own)
        lifted = lax.dot_general(
            one_head(query[:, lo : lo + 128], head % 2),
            wd_ref[:, lo : lo + 128],
            NT,
            preferred_element_type=F32,
        )
        all_ref[pl.ds(head * n, n), :] = (lifted * LOG2E).astype(BF16)
        puts.append(put(head, 1, 2 + head))
    own_ref[...] = own
    puts.append(start_copy(own_ref, own_hbm, out_sems.at[2 + HEADS]))
    for copy in puts:
        copy.wait()


def prep(near, mark, x, gain, wq, wkv, wd):
    n, d = x.shape
    outs = [((16 * n, 256), BF16), ((n, 128), F32)]
    ins = [(v.shape, v.dtype) for v in (x, wq, wkv, wd)]
    return pl.pallas_call(
        prep_kernel,
        out_shape=tuple(shape(*o) for o in outs),
        in_specs=[VMEM, VMEM, HBM, VMEM, HBM, HBM, HBM],
        out_specs=(HBM,) * 2,
        scratch_shapes=[pltpu.VMEM(*v) for v in ins + outs]
        + [
            pltpu.VMEM(near.shape[::-1], jnp.int32),
            pltpu.SemaphoreType.DMA((4,)),
            pltpu.SemaphoreType.DMA((3 + HEADS,)),
        ],
        compiler_params=params(),
        cost_estimate=pl.CostEstimate(flops=8 * 10**9, bytes_accessed=8 * 10**6, transcendentals=0),
        name="prep",
    )(near, mark, x, gain, wq, wkv, wd)


def near_kernel(
    got_hbm, w_hbm, all_hbm, own_hbm, top_hbm, sum_hbm, acc_hbm,
    got_ref, w_ref, query_ref, count_ref, own_ref, value_ref, top_ref, sum_ref, acc_ref,
    key_ref, val_ref, bias_ref, sems,
):
    slots = got_ref.shape[0]
    n, d = query_ref.shape
    get_got = start_copy(got_hbm, got_ref, sems.at[0])
    get_w = start_copy(w_hbm, w_ref, sems.at[1])

    def get_block(block, target, j, sem):
        return start_copy(
            all_hbm.at[pl.ds(block * n, n), :], target.at[:, pl.ds(j * 256, 256)], sems.at[sem]
        )

    get_count = [get_block(12 + j, count_ref, j, 8 + j) for j in range(4)]
    gets = [get_block(8 + j, query_ref, j, 2 + j) for j in range(2)]
    gets += [get_block(10 + j, value_ref, j, 4 + j) for j in range(2)]
    gets.append(start_copy(own_hbm, own_ref, sems.at[6]))
    get_got.wait()
    got = got_ref[...]
    absent = got.astype(F32) > 1024.0
    rows = jnp.where(absent, 0.0, got.astype(F32)).astype(BF16)
    ones = jnp.ones((8, 128), BF16)
    empty = lax.dot_general(
        ones, jnp.where(absent[:, :128], 1.0, 0.0).astype(BF16), NT, preferred_element_type=F32
    )[0:1, :]
    get_w.wait()
    kv = jnp.dot(rows, w_ref[...], preferred_element_type=F32).astype(BF16)
    key_ref[...] = kv[:, :d]
    for pair in range(HEADS // 2):
        lo = d + pair * 128
        val_ref[pair, :, :128] = kv[:, lo : lo + 128]
        val_ref[pair, :, 128:] = jnp.ones((slots, 128), BF16)
    for copy in get_count:
        copy.wait()
    count = count_ref[...].astype(F32)
    bias_ref[...] = jnp.where((count > 0.0) & (empty < 0.5), jnp.log2(jnp.maximum(count, 1.0)), NEG)
    for copy in gets:
        copy.wait()

    def attend(step, exact):
        lane = lax.broadcasted_iota(jnp.int32, (step, 128), 1)

        def body(i, carry):
            at = pl.ds(pl.multiple_of(i * step, step), step)
            own = own_ref[at, :]
            tops = own
            sums = jnp.ones((step, 128), F32)
            for pair in range(HEADS // 2):
                lo = pair * 128
                sides = []
                for odd in range(2):
                    head = 2 * pair + odd
                    scores = lax.dot_general(
                        one_head(query_ref[at, lo : lo + 128], odd),
                        key_ref[:, lo : lo + 128],
                        NT,
                        preferred_element_type=F32,
                    )
                    scores = scores * LOG2E + bias_ref[at, :]
                    shift = own[:, head : head + 1]
                    if exact:
                        mine = shift
                        shift = jnp.maximum(jnp.max(scores, axis=1, keepdims=True), mine)
                        self_weight = jnp.exp2(mine - shift).astype(BF16).astype(F32)
                        tops = jnp.where(lane == head, shift, tops)
                    else:
                        self_weight = 1.0
                    weights = jnp.exp2(scores - shift).astype(BF16)
                    part = jnp.dot(weights, val_ref[pair], preferred_element_type=F32)
                    sums = jnp.where(lane == head, part[:, 128:] + self_weight, sums)
                    sides.append(part[:, :128] + self_weight * value_ref[at, lo : lo + 128].astype(F32))
                acc_ref[at, lo : lo + 128] = jnp.where(lane < 64, sides[0], sides[1])
            top_ref[at, :] = tops
            sum_ref[at, :] = sums
            return carry

        lax.fori_loop(0, n // step, body, 0)

    attend(256, False)
    worst = jnp.max(jnp.max(sum_ref[...], axis=0, keepdims=True))

    @pl.when(jnp.logical_not(worst < BIG))
    def _():
        attend(64, True)

    puts = [
        start_copy(top_ref, top_hbm, sems.at[12]),
        start_copy(sum_ref, sum_hbm, sems.at[13]),
        start_copy(acc_ref, acc_hbm, sems.at[14]),
    ]
    for copy in puts:
        copy.wait()


def near_attend(got, w, everything, own):
    n, d = own.shape[0], w.shape[1] // 2
    slots = got.shape[0]
    ins = [(got.shape, BF16), (w.shape, BF16), ((n, d), BF16), ((n, slots), BF16)]
    ins += [(own.shape, F32), ((n, d), BF16)]
    outs = [((n, 128), F32), ((n, 128), F32), ((n, d), F32)]
    return pl.pallas_call(
        near_kernel,
        out_shape=tuple(shape(*o) for o in outs),
        in_specs=[HBM] * 4,
        out_specs=(HBM,) * 3,
        scratch_shapes=[pltpu.VMEM(*v) for v in ins + outs]
        + [
            pltpu.VMEM((slots, d), BF16),
            pltpu.VMEM((HEADS // 2, slots, 256), BF16),
            pltpu.VMEM((n, slots), F32),
            pltpu.SemaphoreType.DMA((15,)),
        ],
        compiler_params=params(),
        cost_estimate=pl.CostEstimate(flops=5 * 10**9, bytes_accessed=5 * 10**6, transcendentals=10**6),
        name="near_attend",
    )(got, w, everything, own)


def disk_kernel(*refs, pieces):
    (start_ref, extent_ref, lifted_hbm), refs = refs[:3], refs[3:]
    piece_hbm, refs = refs[:pieces], refs[pieces:]
    late_hbm, refs = refs[:7], refs[7:]
    out_ref, own_ref, lifted_ref, tok_ref = refs[:4]
    top_ref, sum_ref, near_ref, wd_ref, wout_ref, x_ref = late_refs = refs[4:10]
    shift_ref, acc_ref, den_ref, att_ref, sems, tok_sems = refs[10:]
    own_hbm = late_hbm[0]
    n, d = x_ref.shape
    rows = lifted_ref.shape[0]
    disks, size = piece_hbm[0].shape[:2]

    get_own = start_copy(own_hbm, own_ref, sems.at[0])
    get_lifted = start_copy(lifted_hbm.at[pl.ds(0, rows), :], lifted_ref, sems.at[1])
    here = lax.axis_index("lon")
    sectors = lax.axis_size("lon")

    def seen(disk):
        return lax.rem(here - start_ref[disk] + sectors, sectors) < extent_ref[disk]

    def token_copies(disk):
        return [
            pltpu.make_async_copy(
                piece_hbm[i].at[disk],
                tok_ref.at[disk, pl.ds(i * size, size), :],
                tok_sems.at[disk, i],
            )
            for i in range(pieces)
        ]

    for disk in range(disks):

        @pl.when(seen(disk))
        def _():
            for copy in token_copies(disk):
                copy.start()

    late = [
        start_copy(source, target, sems.at[2 + i])
        for i, (source, target) in enumerate(zip(late_hbm[1:], late_refs))
    ]

    def add_disks(step, unroll, first):
        den_ref[...] = jnp.zeros_like(den_ref)
        acc_ref[...] = jnp.zeros_like(acc_ref)
        if first:
            get_own.wait()
            for head in range(HEADS):
                shift_ref[pl.ds(head * n, n), :] = jnp.broadcast_to(own_ref[:, head : head + 1], (n, 128))
            get_lifted.wait()
            for disk in range(disks):

                @pl.when(seen(disk))
                def _():
                    for copy in token_copies(disk):
                        copy.wait()

        def add_disk(disk, carry):
            @pl.when(seen(disk))
            def _():
                def body(i, inner):
                    for u in range(unroll):
                        at = pl.ds(pl.multiple_of((i * unroll + u) * step, step), step)
                        scores = lax.dot_general(
                            lifted_ref[at, :], tok_ref[disk], NT, preferred_element_type=F32
                        )
                        weights = jnp.exp2(scores - shift_ref[at, :1])
                        part = weights[:, :128]
                        for j in range(1, weights.shape[1] // 128):
                            part = part + weights[:, j * 128 : j * 128 + 128]
                        den_ref[at, :] += part
                        acc_ref[at, :] += jnp.dot(
                            weights.astype(BF16), tok_ref[disk], preferred_element_type=F32
                        )
                    return inner

                lax.fori_loop(0, rows // (step * unroll), body, 0)

            return carry

        lax.fori_loop(0, disks, add_disk, 0)

    add_disks(256, 8, True)

    worst = jnp.max(jnp.max(den_ref[...], axis=0, keepdims=True))

    @pl.when(jnp.logical_not(worst < BIG))
    def _():
        def top_disk(disk, carry):
            @pl.when(seen(disk))
            def _():
                def body(i, inner):
                    at = pl.ds(pl.multiple_of(i * 128, 128), 128)
                    scores = lax.dot_general(
                        lifted_ref[at, :], tok_ref[disk], NT, preferred_element_type=F32
                    )
                    best = jnp.max(scores, axis=1, keepdims=True)
                    shift_ref[at, :] = jnp.maximum(shift_ref[at, :], best)
                    return inner

                lax.fori_loop(0, rows // 128, body, 0)

            return carry

        lax.fori_loop(0, disks, top_disk, 0)
        add_disks(128, 1, False)

    for copy in late:
        copy.wait()
    lane = lax.broadcasted_iota(jnp.int32, (n, 128), 1)
    for pair in range(HEADS // 2):
        lo = pair * 128
        sides = []
        for odd in range(2):
            head = 2 * pair + odd
            at = pl.ds(head * n, n)
            shift = shift_ref[at, :1]
            top = top_ref[:, head : head + 1]
            best = jnp.maximum(shift, top)
            disk_scale = jnp.exp2(shift - best)
            near_scale = jnp.exp2(top - best)
            total = (
                jnp.sum(den_ref[at, :], axis=1, keepdims=True) * disk_scale
                + sum_ref[:, head : head + 1] * near_scale
            )
            inv = 1.0 / total
            mixed = (acc_ref[at, :] * (disk_scale * inv)).astype(BF16)
            part = jnp.dot(mixed, wd_ref[:, d + lo : d + lo + 128], preferred_element_type=F32)
            sides.append(part + near_ref[:, lo : lo + 128] * (near_scale * inv))
        att_ref[:, lo : lo + 128] = jnp.where(lane < 64, sides[0], sides[1]).astype(BF16)
    out = jnp.dot(att_ref[...], wout_ref[...], preferred_element_type=F32)
    out_ref[...] = (x_ref[...].astype(F32) + out).astype(BF16)


def disk_attend(start, extent, everything, pieces, own, top, total, near, wd, wout, x):
    n, d = x.shape
    disks = pieces[0].shape[0]
    tokens = sum(piece.shape[1] for piece in pieces)
    rows, width = HEADS * n, wd.shape[0]
    late = (top, total, near, wd, wout, x)
    return pl.pallas_call(
        functools.partial(disk_kernel, pieces=len(pieces)),
        out_shape=shape((n, d), BF16),
        in_specs=[SMEM, SMEM] + [HBM] * (8 + len(pieces)),
        out_specs=VMEM,
        scratch_shapes=[
            pltpu.VMEM(own.shape, F32),
            pltpu.VMEM((rows, width), BF16),
            pltpu.VMEM((disks, tokens, width), BF16),
        ]
        + [pltpu.VMEM(v.shape, v.dtype) for v in late]
        + [
            pltpu.VMEM((rows, 128), F32),
            pltpu.VMEM((rows, width), F32),
            pltpu.VMEM((rows, 128), F32),
            pltpu.VMEM((n, d), BF16),
            pltpu.SemaphoreType.DMA((8,)),
            pltpu.SemaphoreType.DMA((disks, len(pieces))),
        ],
        compiler_params=params(),
        cost_estimate=pl.CostEstimate(flops=16 * 10**9, bytes_accessed=10**7, transcendentals=10**6),
        name="disk_attend",
    )(start, extent, everything, *pieces, own, *late)


def device_at(z, y, x, core):
    return (z * 2 + y // 2) * 16 + (y % 2) * 8 + x * 2 + core


def ring(*steps):
    pairs = []
    for z in range(4):
        for y in range(4):
            for x in range(4):
                for core in range(2):
                    axis, by = steps[core]
                    to = [z, y, x]
                    to[axis] = (to[axis] + by) % 4
                    pairs.append((device_at(z, y, x, core), device_at(*to, core)))
    return pairs


def other_core():
    return [(s, s ^ 1) for s in range(128)]


def spread(block, first, second):
    return [lax.ppermute(block, AXES, ring((first, by), (second, by))) for by in (1, 3, 2)]


def gather_tokens(disk_tokens):
    block = jnp.transpose(disk_tokens, (1, 0, 2))
    block = jnp.concatenate([block] + spread(block, 0, 1), axis=1)
    block = jnp.concatenate([block] + spread(block, 1, 2), axis=1)
    pieces = [block] + spread(block, 2, 0)
    return pieces + [lax.ppermute(piece, AXES, other_core()) for piece in pieces]


def local(
    mesh_nodes,
    norm_gain,
    w_query,
    w_node_kv,
    obs_rows,
    w_obs_kv,
    obs_owner,
    neighbours,
    neighbour_mask,
    disk_tokens,
    w_disk_kv,
    disk_start,
    disk_extent,
    w_out,
):
    devices = lax.axis_size("lat") * lax.axis_size("lon")
    width = obs_rows.shape[1]
    slots = devices * 8
    send = place(obs_owner.reshape(1, -1), obs_rows, slots)
    got = lax.all_to_all(
        send.reshape(devices, 8, width), AXES, split_axis=0, concat_axis=0, tiled=True
    ).reshape(slots, width)
    everything, own = prep(
        neighbours.T,
        neighbour_mask.T,
        mesh_nodes,
        norm_gain.reshape(1, -1),
        w_query,
        w_node_kv,
        w_disk_kv,
    )
    pieces = gather_tokens(disk_tokens)
    top, total, near = near_attend(got, w_obs_kv, everything, own)
    return disk_attend(
        disk_start, disk_extent, everything, pieces, own, top, total, near, w_disk_kv, w_out, mesh_nodes
    )


def solution(mesh):
    split = P(AXES, None)
    return jax.shard_map(
        local,
        mesh=mesh,
        in_specs=(
            split,
            P(),
            P(),
            P(),
            split,
            P(),
            split,
            split,
            split,
            P(AXES, None, None),
            P(),
            P(),
            P(),
            P(),
        ),
        out_specs=split,
        check_vma=False,
    )
```

profile of v0, /device:TPU:0, one launch (start us, length us, event | category | flops | bytes accessed | tf_op | source)
XLA Modules:
  0.0 102.1 jit_solution(6387543380152418882)
XLA Ops:
  0.0 4.0 %collective-permute-start.2 = (bf16[5,8,256]{2,1,0:T(8,128)(2,1)}, bf16[5,8,256]{2,1,0:T(8,128)(2,1)}, u32[]{:S(2)}, u32[]{:S(2)}) collective-permute-start(bf16[5,8,256]{2,1,0:T(8,128)(2,1)} %bitcast.10), channel_id=1, source_target_pairs={{0,64},{1,17},{2,66},{3,19},{4,68},{5,21},{6,70},{7,23},{8,72},{9,... | collective-permute-start | bytes 61448 | tf_op jit(solution)/shard_map/ppermute | solution.py:484
  4.0 0.7 collective-permute-start.1
  4.7 1.3 %collective-permute-start = (bf16[5,8,256]{2,1,0:T(8,128)(2,1)}, bf16[5,8,256]{2,1,0:T(8,128)(2,1)}, u32[]{:S(2)}, u32[]{:S(2)}) collective-permute-start(bf16[5,8,256]{2,1,0:T(8,128)(2,1)} %bitcast.12), channel_id=1, source_target_pairs={{0,32},{1,9},{2,34},{3,11},{4,36},{5,13},{6,38},{7,15},{8,40},{9,1... | collective-permute-start | bytes 61448 | tf_op jit(solution)/shard_map/ppermute | solution.py:484
  6.0 2.6 %place.1 = bf16[1024,256]{1,0:T(8,128)(2,1)} custom-call(s32[1,512]{1,0:T(1,128)} %bitcast.16, bf16[512,256]{1,0:T(8,128)(2,1)} %rows_ref.1), custom_call_target="tpu_custom_call" | custom-call | flops 1000000000 | bytes 1000000 | tf_op jit(solution)/shard_map/place/pallas_call | solution.py:70
  8.7 9.0 %all-to-all-start = ((bf16[128,8,256]{2,1,0:T(8,128)(2,1)}), bf16[128,8,256]{2,1,0:T(8,128)(2,1)S(1)}, u32[]{:S(2)}, u32[]{:S(2)}) async-start(bf16[128,8,256]{2,1,0:T(8,128)(2,1)} %bitcast.9), calls=%async_computation | async-start | bytes 1048576 | tf_op jit(solution)/shard_map/all_to_all | solution.py:515
  17.6 0.7 constant_dynamic-update-slice_fusion.6
  18.4 0.8 pad_maximum_fusion
  19.2 2.5 %collective-permute-start.5 = (bf16[5,32,256]{2,1,0:T(8,128)(2,1)S(1)}, bf16[5,32,256]{2,1,0:T(8,128)(2,1)S(1)}, u32[]{:S(2)}, u32[]{:S(2)}) collective-permute-start(bf16[5,32,256]{2,1,0:T(8,128)(2,1)S(1)} %pad_maximum_fusion), channel_id=1, source_target_pairs={{0,16},{1,5},{2,18},{3,7},{4,20},{5,1},{6,22},{7,3},{8,24},{9,13},... | collective-permute-start | bytes 245768 | tf_op jit(solution)/shard_map/ppermute | solution.py:484
  21.7 1.2 %collective-permute-start.4 = (bf16[5,32,256]{2,1,0:T(8,128)(2,1)S(1)}, bf16[5,32,256]{2,1,0:T(8,128)(2,1)S(1)}, u32[]{:S(2)}, u32[]{:S(2)}) collective-permute-start(bf16[5,32,256]{2,1,0:T(8,128)(2,1)S(1)} %pad_maximum_fusion), channel_id=1, source_target_pairs={{0,24},{1,7},{2,26},{3,1},{4,28},{5,3},{6,30},{7,5},{8,0},{9,15},{... | collective-permute-start | bytes 245768 | tf_op jit(solution)/shard_map/ppermute | solution.py:484
  22.9 0.9 collective-permute-start.3
  23.7 0.7 constant_dynamic-update-slice_fusion.5
  24.4 0.7 constant_dynamic-update-slice_fusion.4
  25.2 0.7 constant_dynamic-update-slice_fusion.3
  25.9 2.7 %collective-permute-done.3 = bf16[5,32,256]{2,1,0:T(8,128)(2,1)S(1)} collective-permute-done((bf16[5,32,256]{2,1,0:T(8,128)(2,1)S(1)}, bf16[5,32,256]{2,1,0:T(8,128)(2,1)S(1)}, u32[]{:S(2)}, u32[]{:S(2)}) %collective-permute-start.3) | collective-permute-done | bytes 81952 | tf_op jit(solution)/shard_map/ppermute | solution.py:484
  28.6 3.0 %collective-permute-start.8 = (bf16[5,128,256]{2,1,0:T(8,128)(2,1)S(1)}, bf16[5,128,256]{2,1,0:T(8,128)(2,1)S(1)}, u32[]{:S(2)}, u32[]{:S(2)}) collective-permute-start(bf16[5,128,256]{2,1,0:T(8,128)(2,1)S(1)} %constant_dynamic-update-slice_fusion.refs_3_), channel_id=1, source_target_pairs={{0,4},{1,65},{2,6},{3,67},{4,0},{5,69},{6,2},{7,71},{8,12},{9,73},... | collective-permute-start | bytes 983048 | tf_op jit(solution)/shard_map/ppermute | solution.py:484
  31.6 1.2 %collective-permute-start.7 = (bf16[5,128,256]{2,1,0:T(8,128)(2,1)S(1)}, bf16[5,128,256]{2,1,0:T(8,128)(2,1)S(1)}, u32[]{:S(2)}, u32[]{:S(2)}) collective-permute-start(bf16[5,128,256]{2,1,0:T(8,128)(2,1)S(1)} %constant_dynamic-update-slice_fusion.refs_3_), channel_id=1, source_target_pairs={{0,6},{1,97},{2,0},{3,99},{4,2},{5,101},{6,4},{7,103},{8,14},{9,10... | collective-permute-start | bytes 983048 | tf_op jit(solution)/shard_map/ppermute | solution.py:484
  32.8 0.8 collective-permute-start.6
  33.6 8.4 %prep.1 = (bf16[8192,256]{1,0:T(8,128)(2,1)}, f32[512,128]{1,0:T(8,128)}) custom-call(s32[32,512]{1,0:T(8,128)} %bitcast.14, s32[32,512]{1,0:T(8,128)} %bitcast.15, bf16[512,512]{1,0:T(8,128)(2,1)} %refs_17_.1, f32[1,512]{1,0:T(1,128)} %bitcast.17, bf16[512,512]{1,0:T(8,128)(2,1)} %wq_hbm.1, bf16[512,1024]{1,0:T(8,128)(2,1)} %wkv_hbm.1, ...), custom_call_target="tpu_custom_call" | custom-call | flops 8000000000 | bytes 8000000 | tf_op jit(solution)/shard_map/prep/pallas_call | solution.py:160
  42.2 0.5 collective-permute-start.12
  42.8 0.4 collective-permute-start.10
  43.2 0.8 copy-done
  44.0 25.8 %near_attend.1 = (f32[512,128]{1,0:T(8,128)}, f32[512,128]{1,0:T(8,128)}, f32[512,512]{1,0:T(8,128)}) custom-call(bf16[1024,256]{1,0:T(8,128)(2,1)} %bitcast.8, bf16[256,1024]{1,0:T(8,128)(2,1)} %w_hbm.1, bf16[8192,256]{1,0:T(8,128)(2,1)} %get-tuple-element.10.all_hbm.refs_2_, f32[512,128]{1,0:T(8,128)} %get-tuple-element.11.own_hbm.refs_11_), custom_call_target="tpu_custom_call" | custom-call | flops 5000000000 | bytes 5000000 | tf_op jit(solution)/shard_map/near_attend/pallas_call | solution.py:279
  70.0 0.6 copy-done.5
  70.9 31.0 %disk_attend.1 = bf16[512,512]{1,0:T(8,128)(2,1)} custom-call(s32[5]{0:T(128)} %refs_0_.1, s32[5]{0:T(128)} %refs_1_.1, bf16[8192,256]{1,0:T(8,128)(2,1)} %get-tuple-element.10.all_hbm.refs_2_, bf16[5,128,256]{2,1,0:T(8,128)(2,1)} %copy-done.1, bf16[5,128,256]{2,1,0:T(8,128)(2,1)} %copy-done.4, bf16[5,128,256]{2,1,0:T(8,128)(2,1)} %copy-done.3, ...), custom_call_target="tpu_custom_call" | custom-call | flops 16000000000 | bytes 10000000 | tf_op jit(solution)/shard_map/disk_attend/pallas_call | solution.py:437
  (34 shorter events, 0.6 us)
Async XLA Ops:
  0.0 18.4 %collective-permute-start.2 = (bf16[5,8,256]{2,1,0:T(8,128)(2,1)}, bf16[5,8,256]{2,1,0:T(8,128)(2,1)}, u32[]{:S(2)}, u32[]{:S(2)}) collective-permute-start(bf16[5,8,256]{2,1,0:T(8,128)(2,1)} %bitcast.10), channel_id=1, source_target_pairs={{0,64},{1,17},{2,66},{3,19},{4,68},{5,21},{6,70},{7,23},{8,72},{9,... | collective-permute-start | bytes 61448 | tf_op jit(solution)/shard_map/ppermute | solution.py:484
  4.0 14.4 %collective-permute-start.1 = (bf16[5,8,256]{2,1,0:T(8,128)(2,1)}, bf16[5,8,256]{2,1,0:T(8,128)(2,1)}, u32[]{:S(2)}, u32[]{:S(2)}) collective-permute-start(bf16[5,8,256]{2,1,0:T(8,128)(2,1)} %bitcast.11), channel_id=1, source_target_pairs={{0,96},{1,25},{2,98},{3,27},{4,100},{5,29},{6,102},{7,31},{8,104},... | collective-permute-start | bytes 61448 | tf_op jit(solution)/shard_map/ppermute | solution.py:484
  4.7 13.7 %collective-permute-start = (bf16[5,8,256]{2,1,0:T(8,128)(2,1)}, bf16[5,8,256]{2,1,0:T(8,128)(2,1)}, u32[]{:S(2)}, u32[]{:S(2)}) collective-permute-start(bf16[5,8,256]{2,1,0:T(8,128)(2,1)} %bitcast.12), channel_id=1, source_target_pairs={{0,32},{1,9},{2,34},{3,11},{4,36},{5,13},{6,38},{7,15},{8,40},{9,1... | collective-permute-start | bytes 61448 | tf_op jit(solution)/shard_map/ppermute | solution.py:484
  8.7 34.6 %all-to-all-start = ((bf16[128,8,256]{2,1,0:T(8,128)(2,1)}), bf16[128,8,256]{2,1,0:T(8,128)(2,1)S(1)}, u32[]{:S(2)}, u32[]{:S(2)}) async-start(bf16[128,8,256]{2,1,0:T(8,128)(2,1)} %bitcast.9), calls=%async_computation | async-start | bytes 1048576 | tf_op jit(solution)/shard_map/all_to_all | solution.py:515
  19.2 9.4 %collective-permute-start.5 = (bf16[5,32,256]{2,1,0:T(8,128)(2,1)S(1)}, bf16[5,32,256]{2,1,0:T(8,128)(2,1)S(1)}, u32[]{:S(2)}, u32[]{:S(2)}) collective-permute-start(bf16[5,32,256]{2,1,0:T(8,128)(2,1)S(1)} %pad_maximum_fusion), channel_id=1, source_target_pairs={{0,16},{1,5},{2,18},{3,7},{4,20},{5,1},{6,22},{7,3},{8,24},{9,13},... | collective-permute-start | bytes 245768 | tf_op jit(solution)/shard_map/ppermute | solution.py:484
  21.7 6.9 %collective-permute-start.4 = (bf16[5,32,256]{2,1,0:T(8,128)(2,1)S(1)}, bf16[5,32,256]{2,1,0:T(8,128)(2,1)S(1)}, u32[]{:S(2)}, u32[]{:S(2)}) collective-permute-start(bf16[5,32,256]{2,1,0:T(8,128)(2,1)S(1)} %pad_maximum_fusion), channel_id=1, source_target_pairs={{0,24},{1,7},{2,26},{3,1},{4,28},{5,3},{6,30},{7,5},{8,0},{9,15},{... | collective-permute-start | bytes 245768 | tf_op jit(solution)/shard_map/ppermute | solution.py:484
  22.9 5.7 %collective-permute-start.3 = (bf16[5,32,256]{2,1,0:T(8,128)(2,1)S(1)}, bf16[5,32,256]{2,1,0:T(8,128)(2,1)S(1)}, u32[]{:S(2)}, u32[]{:S(2)}) collective-permute-start(bf16[5,32,256]{2,1,0:T(8,128)(2,1)S(1)} %pad_maximum_fusion), channel_id=1, source_target_pairs={{0,8},{1,3},{2,10},{3,5},{4,12},{5,7},{6,14},{7,1},{8,16},{9,11},{... | collective-permute-start | bytes 245768 | tf_op jit(solution)/shard_map/ppermute | solution.py:484
  28.6 13.5 %copy-start.1 = (bf16[5,128,256]{2,1,0:T(8,128)(2,1)}, bf16[5,128,256]{2,1,0:T(8,128)(2,1)S(1)}, u32[]{:S(2)}) copy-start(bf16[5,128,256]{2,1,0:T(8,128)(2,1)S(1)} %constant_dynamic-update-slice_fusion.refs_3_) | copy-start | bytes 983044
  28.6 13.6 %collective-permute-start.8 = (bf16[5,128,256]{2,1,0:T(8,128)(2,1)S(1)}, bf16[5,128,256]{2,1,0:T(8,128)(2,1)S(1)}, u32[]{:S(2)}, u32[]{:S(2)}) collective-permute-start(bf16[5,128,256]{2,1,0:T(8,128)(2,1)S(1)} %constant_dynamic-update-slice_fusion.refs_3_), channel_id=1, source_target_pairs={{0,4},{1,65},{2,6},{3,67},{4,0},{5,69},{6,2},{7,71},{8,12},{9,73},... | collective-permute-start | bytes 983048 | tf_op jit(solution)/shard_map/ppermute | solution.py:484
  31.6 11.1 %collective-permute-start.7 = (bf16[5,128,256]{2,1,0:T(8,128)(2,1)S(1)}, bf16[5,128,256]{2,1,0:T(8,128)(2,1)S(1)}, u32[]{:S(2)}, u32[]{:S(2)}) collective-permute-start(bf16[5,128,256]{2,1,0:T(8,128)(2,1)S(1)} %constant_dynamic-update-slice_fusion.refs_3_), channel_id=1, source_target_pairs={{0,6},{1,97},{2,0},{3,99},{4,2},{5,101},{6,4},{7,103},{8,14},{9,10... | collective-permute-start | bytes 983048 | tf_op jit(solution)/shard_map/ppermute | solution.py:484
  32.8 10.0 %collective-permute-start.6 = (bf16[5,128,256]{2,1,0:T(8,128)(2,1)S(1)}, bf16[5,128,256]{2,1,0:T(8,128)(2,1)S(1)}, u32[]{:S(2)}, u32[]{:S(2)}) collective-permute-start(bf16[5,128,256]{2,1,0:T(8,128)(2,1)S(1)} %constant_dynamic-update-slice_fusion.refs_3_), channel_id=1, source_target_pairs={{0,2},{1,33},{2,4},{3,35},{4,6},{5,37},{6,0},{7,39},{8,10},{9,41},... | collective-permute-start | bytes 983048 | tf_op jit(solution)/shard_map/ppermute | solution.py:484
  42.1 27.8 %collective-permute-start.9 = (bf16[5,128,256]{2,1,0:T(8,128)(2,1)S(1)}, bf16[5,128,256]{2,1,0:T(8,128)(2,1)S(1)}, u32[]{:S(2)}, u32[]{:S(2)}) collective-permute-start(bf16[5,128,256]{2,1,0:T(8,128)(2,1)S(1)} %constant_dynamic-update-slice_fusion.refs_3_), channel_id=1, source_target_pairs={{0,1},{1,0},{2,3},{3,2},{4,5},{5,4},{6,7},{7,6},{8,9},{9,8},{10,11... | collective-permute-start | bytes 983048 | tf_op jit(solution)/shard_map/ppermute | solution.py:492
  42.2 27.7 %copy-start.2 = (bf16[5,128,256]{2,1,0:T(8,128)(2,1)}, bf16[5,128,256]{2,1,0:T(8,128)(2,1)S(1)}, u32[]{:S(2)}) copy-start(bf16[5,128,256]{2,1,0:T(8,128)(2,1)S(1)} %collective-permute-done.8.refs_6_) | copy-start | bytes 983044
  42.2 27.7 %collective-permute-start.12 = (bf16[5,128,256]{2,1,0:T(8,128)(2,1)S(1)}, bf16[5,128,256]{2,1,0:T(8,128)(2,1)S(1)}, u32[]{:S(2)}, u32[]{:S(2)}) collective-permute-start(bf16[5,128,256]{2,1,0:T(8,128)(2,1)S(1)} %collective-permute-done.8.refs_6_), channel_id=1, source_target_pairs={{0,1},{1,0},{2,3},{3,2},{4,5},{5,4},{6,7},{7,6},{8,9},{9,8},{10,11... | collective-permute-start | bytes 983048 | tf_op jit(solution)/shard_map/ppermute | solution.py:492
  42.7 27.2 %copy-start.3 = (bf16[5,128,256]{2,1,0:T(8,128)(2,1)}, bf16[5,128,256]{2,1,0:T(8,128)(2,1)S(1)}, u32[]{:S(2)}) copy-start(bf16[5,128,256]{2,1,0:T(8,128)(2,1)S(1)} %collective-permute-done.7.refs_5_) | copy-start | bytes 983044
  42.7 27.2 %collective-permute-start.11 = (bf16[5,128,256]{2,1,0:T(8,128)(2,1)S(1)}, bf16[5,128,256]{2,1,0:T(8,128)(2,1)S(1)}, u32[]{:S(2)}, u32[]{:S(2)}) collective-permute-start(bf16[5,128,256]{2,1,0:T(8,128)(2,1)S(1)} %collective-permute-done.7.refs_5_), channel_id=1, source_target_pairs={{0,1},{1,0},{2,3},{3,2},{4,5},{5,4},{6,7},{7,6},{8,9},{9,8},{10,11... | collective-permute-start | bytes 983048 | tf_op jit(solution)/shard_map/ppermute | solution.py:492
  42.8 27.1 %copy-start.4 = (bf16[5,128,256]{2,1,0:T(8,128)(2,1)}, bf16[5,128,256]{2,1,0:T(8,128)(2,1)S(1)}, u32[]{:S(2)}) copy-start(bf16[5,128,256]{2,1,0:T(8,128)(2,1)S(1)} %collective-permute-done.6.refs_4_) | copy-start | bytes 983044
  42.8 27.1 %collective-permute-start.10 = (bf16[5,128,256]{2,1,0:T(8,128)(2,1)S(1)}, bf16[5,128,256]{2,1,0:T(8,128)(2,1)S(1)}, u32[]{:S(2)}, u32[]{:S(2)}) collective-permute-start(bf16[5,128,256]{2,1,0:T(8,128)(2,1)S(1)} %collective-permute-done.6.refs_4_), channel_id=1, source_target_pairs={{0,1},{1,0},{2,3},{3,2},{4,5},{5,4},{6,7},{7,6},{8,9},{9,8},{10,11... | collective-permute-start | bytes 983048 | tf_op jit(solution)/shard_map/ppermute | solution.py:492
  43.2 0.8 copy-start
  69.9 0.7 copy-start.5
  69.9 0.8 copy-start.6
  69.9 0.9 copy-start.7
  69.9 1.0 copy-start.8
where the time goes:
time: 103 us; the launch traced here: 102 us
  Pallas kernels  67.9 us (66%)
  starting transfers between devices  25.6 us (25%)
  local copies, waits for them, and re-layouts  4.71 us (5%)
  waiting for transfers between devices  2.69 us (3%)
    pallas_call x1, Pallas kernels, disk_attend(): pl.pallas_call(functools.partial(disk_kernel, pieces=len(pieces)), out_sh...  31 us
    pallas_call x1, Pallas kernels, near_attend(): pl.pallas_call(near_kernel, out_shape=tuple((shape(*o) for o in outs)), i...  25.8 us
    ppermute x9, starting transfers between devices, spread(): lax.ppermute(block, AXES, ring((first, by), (second, by)))  15.6 us
    all_to_all x1, starting transfers between devices, local(): lax.all_to_all(send.reshape(devices, 8, width), AXES, split_axis=0, conca...  8.95 us
    pallas_call x1, Pallas kernels, prep(): pl.pallas_call(prep_kernel, out_shape=tuple((shape(*o) for o in outs)), i...  8.43 us
    unnamed x24, local copies, waits for them, and re-layouts  4.71 us
    ppermute x9, waiting for transfers between devices, spread(): lax.ppermute(block, AXES, ring((first, by), (second, by)))  2.68 us
    pallas_call x1, Pallas kernels, place(): pl.pallas_call(place_kernel, out_shape=shape((slots, rows.shape[1]), BF16...  2.64 us
  transfers between devices with their start and end apart: 14, of which 1 were waited for; matrix products, arithmetic and copies ran while one was open for 4% of the time, Pallas kernels for 36%

commit v1 on v0

--- a/solution.py
+++ b/solution.py
@@ -6,6 +6,7 @@
 from jax.experimental import pallas as pl
 from jax.experimental.pallas import tpu as pltpu
 from jax.sharding import PartitionSpec as P
+
 
 HEADS = 8
 AXES = ("lat", "lon")
@@ -154,7 +155,7 @@
 
 
 def prep(near, mark, x, gain, wq, wkv, wd):
-    n, d = x.shape
+    n, _ = x.shape
     outs = [((16 * n, 256), BF16), ((n, 128), F32)]
     ins = [(v.shape, v.dtype) for v in (x, wq, wkv, wd)]
     return pl.pallas_call(
@@ -288,7 +289,7 @@
             pltpu.VMEM((n, slots), F32),
             pltpu.SemaphoreType.DMA((15,)),
         ],
-        compiler_params=params(),
+        compiler_params=params(67043328),
         cost_estimate=pl.CostEstimate(flops=5 * 10**9, bytes_accessed=5 * 10**6, transcendentals=10**6),
         name="near_attend",
     )(got, w, everything, own)
@@ -453,7 +454,7 @@
             pltpu.SemaphoreType.DMA((8,)),
             pltpu.SemaphoreType.DMA((disks, len(pieces))),
         ],
-        compiler_params=params(),
+        compiler_params=params(67043328),
         cost_estimate=pl.CostEstimate(flops=16 * 10**9, bytes_accessed=10**7, transcendentals=10**6),
         name="disk_attend",
     )(start, extent, everything, *pieces, own, *late)
@@ -481,15 +482,23 @@
 
 
 def spread(block, first, second):
-    return [lax.ppermute(block, AXES, ring((first, by), (second, by))) for by in (1, 3, 2)]
+    got = []
+    for by in (1, 3, 2):
+        got.append(lax.ppermute(block, AXES, ring((first, by), (second, by))))
+    return got
 
 
 def gather_tokens(disk_tokens):
     block = jnp.transpose(disk_tokens, (1, 0, 2))
     block = jnp.concatenate([block] + spread(block, 0, 1), axis=1)
+    block = lax.optimization_barrier(block)
     block = jnp.concatenate([block] + spread(block, 1, 2), axis=1)
+    block = lax.optimization_barrier(block)
     pieces = [block] + spread(block, 2, 0)
-    return pieces + [lax.ppermute(piece, AXES, other_core()) for piece in pieces]
+    swapped = []
+    for piece in pieces:
+        swapped.append(lax.ppermute(piece, AXES, other_core()))
+    return pieces + swapped
 
 
 def local(

time: 103 us -> 101 us (0.981); the launches traced: 102 us -> 101 us
  local copies, waits for them, and re-layouts: 4.71 us -> 0 us
  other arithmetic: 0.79 us -> 3.13 us
  waiting for transfers between devices: 2.69 us -> 3.92 us
    unnamed x24 -> x0, local copies, waits for them, and re-layouts: 4.71 us -> none
    concatenate x0 -> x1, other arithmetic: none -> 1.76 us  [gather_tokens(): block = jnp.concatenate([block] + spread(block, 1, 2), axis=1)]
    ppermute x13, starting transfers between devices: 16.7 us -> 18.1 us  [the longest x9 15.7 us: spread(): got.append(lax.ppermute(block, AXES, ring((first, by), (second, by))))]
    ppermute x13, waiting for transfers between devices: 2.69 us -> 3.92 us  [the longest x9 3.91 us: spread(): got.append(lax.ppermute(block, AXES, ring((first, by), (second, by))))]
    all_to_all x1, starting transfers between devices: 8.95 us -> 7.8 us  [local(): lax.all_to_all(send.reshape(devices, 8, width), AXES, split_axis=0, conca...]
  transfers between devices with their start and end apart: 14 -> 14, of which waited for: 1 -> 2; matrix products, arithmetic and copies ran while one was open for 4% -> 2% of each run, Pallas kernels for 36% -> 36%
where the time goes in v1:
time: 101 us
  Pallas kernels  67.9 us (67%)
  starting transfers between devices  25.9 us (26%)
  waiting for transfers between devices  3.92 us (4%)
  other arithmetic  3.13 us (3%)
    pallas_call x1, Pallas kernels, disk_attend(): pl.pallas_call(functools.partial(disk_kernel, pieces=len(pieces)), out_sh...  31 us
    pallas_call x1, Pallas kernels, near_attend(): pl.pallas_call(near_kernel, out_shape=tuple((shape(*o) for o in outs)), i...  25.8 us
    ppermute x9, starting transfers between devices, spread(): got.append(lax.ppermute(block, AXES, ring((first, by), (second, by))))  15.7 us
    pallas_call x1, Pallas kernels, prep(): pl.pallas_call(prep_kernel, out_shape=tuple((shape(*o) for o in outs)), i...  8.44 us
    all_to_all x1, starting transfers between devices, local(): lax.all_to_all(send.reshape(devices, 8, width), AXES, split_axis=0, conca...  7.8 us
    ppermute x9, waiting for transfers between devices, spread(): got.append(lax.ppermute(block, AXES, ring((first, by), (second, by))))  3.91 us
    pallas_call x1, Pallas kernels, place(): pl.pallas_call(place_kernel, out_shape=shape((slots, rows.shape[1]), BF16...  2.64 us
    ppermute x4, starting transfers between devices, gather_tokens(): swapped.append(lax.ppermute(piece, AXES, other_core()))  2.42 us
  transfers between devices with their start and end apart: 14, of which 2 were waited for; matrix products, arithmetic and copies ran while one was open for 2% of the time, Pallas kernels for 36%

profile of v1, /device:TPU:0, one launch (start us, length us, event | category | flops | bytes accessed | tf_op | source)
XLA Modules:
  0.0 101.2 jit_solution(9422285063785588004)
XLA Ops:
  0.0 4.0 %collective-permute-start.2 = (bf16[5,8,256]{2,1,0:T(8,128)(2,1)}, bf16[5,8,256]{2,1,0:T(8,128)(2,1)S(1)}, u32[]{:S(2)}, u32[]{:S(2)}) collective-permute-start(bf16[5,8,256]{2,1,0:T(8,128)(2,1)} %bitcast.8), channel_id=1, source_target_pairs={{0,64},{1,17},{2,66},{3,19},{4,68},{5,21},{6,70},{7,23},{8,72},{9,... | collective-permute-start | bytes 61448 | tf_op jit(solution)/shard_map/ppermute | solution.py:487
  4.0 0.7 collective-permute-start.1
  4.7 1.3 %collective-permute-start = (bf16[5,8,256]{2,1,0:T(8,128)(2,1)}, bf16[5,8,256]{2,1,0:T(8,128)(2,1)S(1)}, u32[]{:S(2)}, u32[]{:S(2)}) collective-permute-start(bf16[5,8,256]{2,1,0:T(8,128)(2,1)} %bitcast.10), channel_id=1, source_target_pairs={{0,32},{1,9},{2,34},{3,11},{4,36},{5,13},{6,38},{7,15},{8,40},{9,1... | collective-permute-start | bytes 61448 | tf_op jit(solution)/shard_map/ppermute | solution.py:487
  6.0 0.0 collective-permute-done.2
  6.0 2.0 %collective-permute-done.1 = bf16[5,8,256]{2,1,0:T(8,128)(2,1)S(1)} collective-permute-done((bf16[5,8,256]{2,1,0:T(8,128)(2,1)}, bf16[5,8,256]{2,1,0:T(8,128)(2,1)S(1)}, u32[]{:S(2)}, u32[]{:S(2)}) %collective-permute-start.1) | collective-permute-done | bytes 20512 | tf_op jit(solution)/shard_map/ppermute | solution.py:487
  8.0 1.9 %collective-permute-done = bf16[5,8,256]{2,1,0:T(8,128)(2,1)S(1)} collective-permute-done((bf16[5,8,256]{2,1,0:T(8,128)(2,1)}, bf16[5,8,256]{2,1,0:T(8,128)(2,1)S(1)}, u32[]{:S(2)}, u32[]{:S(2)}) %collective-permute-start) | collective-permute-done | bytes 20512 | tf_op jit(solution)/shard_map/ppermute | solution.py:487
  9.9 1.4 %pad_maximum_fusion.1 = bf16[5,32,256]{2,1,0:T(8,128)(2,1)} fusion(bf16[5,8,256]{2,1,0:T(8,128)(2,1)S(1)} %collective-permute-done.2, bf16[5,8,256]{2,1,0:T(8,128)(2,1)S(1)} %collective-permute-done.1, bf16[5,8,256]{2,1,0:T(8,128)(2,1)S(1)} %collective-permute-done, bf16[5,8,256]{2,1,0:T(8,128)(2,1)} %bitcast.11), kind=kLoop, calls=%fused_computation.1 | loop fusion | flops 327680 | bytes 163840 | tf_op jit(solution)/shard_map/concatenate | solution.py:493
  11.3 3.2 %collective-permute-start.5 = (bf16[5,32,256]{2,1,0:T(8,128)(2,1)}, bf16[5,32,256]{2,1,0:T(8,128)(2,1)}, u32[]{:S(2)}, u32[]{:S(2)}) collective-permute-start(bf16[5,32,256]{2,1,0:T(8,128)(2,1)} %pad_maximum_fusion.1), channel_id=1, source_target_pairs={{0,16},{1,5},{2,18},{3,7},{4,20},{5,1},{6,22},{7,3},{8,24},{9,13},... | collective-permute-start | bytes 245768 | tf_op jit(solution)/shard_map/ppermute | solution.py:487
  14.5 1.1 %collective-permute-start.4 = (bf16[5,32,256]{2,1,0:T(8,128)(2,1)}, bf16[5,32,256]{2,1,0:T(8,128)(2,1)}, u32[]{:S(2)}, u32[]{:S(2)}) collective-permute-start(bf16[5,32,256]{2,1,0:T(8,128)(2,1)} %pad_maximum_fusion.1), channel_id=1, source_target_pairs={{0,24},{1,7},{2,26},{3,1},{4,28},{5,3},{6,30},{7,5},{8,0},{9,15},{... | collective-permute-start | bytes 245768 | tf_op jit(solution)/shard_map/ppermute | solution.py:487
  15.5 1.0 collective-permute-start.3
  16.5 2.6 %place.1 = bf16[1024,256]{1,0:T(8,128)(2,1)} custom-call(s32[1,512]{1,0:T(1,128)} %bitcast.14, bf16[512,256]{1,0:T(8,128)(2,1)} %rows_ref.1), custom_call_target="tpu_custom_call" | custom-call | flops 1000000000 | bytes 1000000 | tf_op jit(solution)/shard_map/place/pallas_call | solution.py:71
  19.1 7.8 %all-to-all-start = ((bf16[128,8,256]{2,1,0:T(8,128)(2,1)}), bf16[128,8,256]{2,1,0:T(8,128)(2,1)}, u32[]{:S(2)}, u32[]{:S(2)}) async-start(bf16[128,8,256]{2,1,0:T(8,128)(2,1)} %bitcast.7), calls=%async_computation | async-start | bytes 1048576 | tf_op jit(solution)/shard_map/all_to_all | solution.py:524
  27.0 0.0 collective-permute-done.5
  27.0 1.8 %pad_maximum_fusion.refs_3_ = bf16[5,128,256]{2,1,0:T(8,128)(2,1)} fusion(bf16[5,32,256]{2,1,0:T(8,128)(2,1)} %collective-permute-done.5, bf16[5,32,256]{2,1,0:T(8,128)(2,1)} %collective-permute-done.4, bf16[5,32,256]{2,1,0:T(8,128)(2,1)} %collective-permute-done.3, bf16[5,32,256]{2,1,0:T(8,128)(2,1)} %pad_maximum_fusion.1), kind=kLoop, calls=%fused_computation | loop fusion | flops 1310720 | bytes 655360 | tf_op jit(solution)/shard_map/concatenate | solution.py:495
  28.7 2.4 %collective-permute-start.8 = (bf16[5,128,256]{2,1,0:T(8,128)(2,1)}, bf16[5,128,256]{2,1,0:T(8,128)(2,1)}, u32[]{:S(2)}, u32[]{:S(2)}) collective-permute-start(bf16[5,128,256]{2,1,0:T(8,128)(2,1)} %pad_maximum_fusion.refs_3_), channel_id=1, source_target_pairs={{0,4},{1,65},{2,6},{3,67},{4,0},{5,69},{6,2},{7,71},{8,12},{9,73},... | collective-permute-start | bytes 983048 | tf_op jit(solution)/shard_map/ppermute | solution.py:487
  31.1 1.2 %collective-permute-start.7 = (bf16[5,128,256]{2,1,0:T(8,128)(2,1)}, bf16[5,128,256]{2,1,0:T(8,128)(2,1)}, u32[]{:S(2)}, u32[]{:S(2)}) collective-permute-start(bf16[5,128,256]{2,1,0:T(8,128)(2,1)} %pad_maximum_fusion.refs_3_), channel_id=1, source_target_pairs={{0,6},{1,97},{2,0},{3,99},{4,2},{5,101},{6,4},{7,103},{8,14},{9,10... | collective-permute-start | bytes 983048 | tf_op jit(solution)/shard_map/ppermute | solution.py:487
  32.3 0.9 collective-permute-start.6
  33.2 8.4 %prep.1 = (bf16[8192,256]{1,0:T(8,128)(2,1)}, f32[512,128]{1,0:T(8,128)}) custom-call(s32[32,512]{1,0:T(8,128)} %bitcast.12, s32[32,512]{1,0:T(8,128)} %bitcast.13, bf16[512,512]{1,0:T(8,128)(2,1)} %refs_17_.1, f32[1,512]{1,0:T(1,128)} %bitcast.15, bf16[512,512]{1,0:T(8,128)(2,1)} %wq_hbm.1, bf16[512,1024]{1,0:T(8,128)(2,1)} %wkv_hbm.1, ...), custom_call_target="tpu_custom_call" | custom-call | flops 8000000000 | bytes 8000000 | tf_op jit(solution)/shard_map/prep/pallas_call | solution.py:161
  41.6 0.1 collective-permute-start.9
  41.7 0.5 collective-permute-start.12
  42.2 0.4 collective-permute-start.11
  42.7 1.4 %collective-permute-start.10 = (bf16[5,128,256]{2,1,0:T(8,128)(2,1)}, bf16[5,128,256]{2,1,0:T(8,128)(2,1)}, u32[]{:S(2)}, u32[]{:S(2)}) collective-permute-start(bf16[5,128,256]{2,1,0:T(8,128)(2,1)} %collective-permute-done.6.refs_4_), channel_id=1, source_target_pairs={{0,1},{1,0},{2,3},{3,2},{4,5},{5,4},{6,7},{7,6},{8,9},{9,8},{10,11... | collective-permute-start | bytes 983048 | tf_op jit(solution)/shard_map/ppermute | solution.py:500
  44.1 25.8 %near_attend.1 = (f32[512,128]{1,0:T(8,128)}, f32[512,128]{1,0:T(8,128)}, f32[512,512]{1,0:T(8,128)}) custom-call(bf16[1024,256]{1,0:T(8,128)(2,1)} %bitcast.6.got_hbm, bf16[256,1024]{1,0:T(8,128)(2,1)} %w_hbm.1, bf16[8192,256]{1,0:T(8,128)(2,1)} %get-tuple-element.10.all_hbm.refs_2_, f32[512,128]{1,0:T(8,128)} %get-tuple-element.11.own_hbm.refs_11_), custom_call_target="tpu_custom_call" | custom-call | flops 5000000000 | bytes 5000000 | tf_op jit(solution)/shard_map/near_attend/pallas_call | solution.py:280
  69.9 31.0 %disk_attend.1 = bf16[512,512]{1,0:T(8,128)(2,1)} custom-call(s32[5]{0:T(128)} %refs_0_.1, s32[5]{0:T(128)} %refs_1_.1, bf16[8192,256]{1,0:T(8,128)(2,1)} %get-tuple-element.10.all_hbm.refs_2_, bf16[5,128,256]{2,1,0:T(8,128)(2,1)} %pad_maximum_fusion.refs_3_, bf16[5,128,256]{2,1,0:T(8,128)(2,1)} %collective-permute-done.6.refs_4_, ...), custom_call_target="tpu_custom_call" | custom-call | flops 16000000000 | bytes 10000000 | tf_op jit(solution)/shard_map/disk_attend/pallas_call | solution.py:438
  (10 shorter events, 0.0 us)
Async XLA Ops:
  0.0 6.0 %collective-permute-start.2 = (bf16[5,8,256]{2,1,0:T(8,128)(2,1)}, bf16[5,8,256]{2,1,0:T(8,128)(2,1)S(1)}, u32[]{:S(2)}, u32[]{:S(2)}) collective-permute-start(bf16[5,8,256]{2,1,0:T(8,128)(2,1)} %bitcast.8), channel_id=1, source_target_pairs={{0,64},{1,17},{2,66},{3,19},{4,68},{5,21},{6,70},{7,23},{8,72},{9,... | collective-permute-start | bytes 61448 | tf_op jit(solution)/shard_map/ppermute | solution.py:487
  4.0 4.0 %collective-permute-start.1 = (bf16[5,8,256]{2,1,0:T(8,128)(2,1)}, bf16[5,8,256]{2,1,0:T(8,128)(2,1)S(1)}, u32[]{:S(2)}, u32[]{:S(2)}) collective-permute-start(bf16[5,8,256]{2,1,0:T(8,128)(2,1)} %bitcast.9), channel_id=1, source_target_pairs={{0,96},{1,25},{2,98},{3,27},{4,100},{5,29},{6,102},{7,31},{8,104},... | collective-permute-start | bytes 61448 | tf_op jit(solution)/shard_map/ppermute | solution.py:487
  4.7 5.2 %collective-permute-start = (bf16[5,8,256]{2,1,0:T(8,128)(2,1)}, bf16[5,8,256]{2,1,0:T(8,128)(2,1)S(1)}, u32[]{:S(2)}, u32[]{:S(2)}) collective-permute-start(bf16[5,8,256]{2,1,0:T(8,128)(2,1)} %bitcast.10), channel_id=1, source_target_pairs={{0,32},{1,9},{2,34},{3,11},{4,36},{5,13},{6,38},{7,15},{8,40},{9,1... | collective-permute-start | bytes 61448 | tf_op jit(solution)/shard_map/ppermute | solution.py:487
  11.3 15.7 %collective-permute-start.5 = (bf16[5,32,256]{2,1,0:T(8,128)(2,1)}, bf16[5,32,256]{2,1,0:T(8,128)(2,1)}, u32[]{:S(2)}, u32[]{:S(2)}) collective-permute-start(bf16[5,32,256]{2,1,0:T(8,128)(2,1)} %pad_maximum_fusion.1), channel_id=1, source_target_pairs={{0,16},{1,5},{2,18},{3,7},{4,20},{5,1},{6,22},{7,3},{8,24},{9,13},... | collective-permute-start | bytes 245768 | tf_op jit(solution)/shard_map/ppermute | solution.py:487
  14.5 12.5 %collective-permute-start.4 = (bf16[5,32,256]{2,1,0:T(8,128)(2,1)}, bf16[5,32,256]{2,1,0:T(8,128)(2,1)}, u32[]{:S(2)}, u32[]{:S(2)}) collective-permute-start(bf16[5,32,256]{2,1,0:T(8,128)(2,1)} %pad_maximum_fusion.1), channel_id=1, source_target_pairs={{0,24},{1,7},{2,26},{3,1},{4,28},{5,3},{6,30},{7,5},{8,0},{9,15},{... | collective-permute-start | bytes 245768 | tf_op jit(solution)/shard_map/ppermute | solution.py:487
  15.5 11.4 %collective-permute-start.3 = (bf16[5,32,256]{2,1,0:T(8,128)(2,1)}, bf16[5,32,256]{2,1,0:T(8,128)(2,1)}, u32[]{:S(2)}, u32[]{:S(2)}) collective-permute-start(bf16[5,32,256]{2,1,0:T(8,128)(2,1)} %pad_maximum_fusion.1), channel_id=1, source_target_pairs={{0,8},{1,3},{2,10},{3,5},{4,12},{5,7},{6,14},{7,1},{8,16},{9,11},{... | collective-permute-start | bytes 245768 | tf_op jit(solution)/shard_map/ppermute | solution.py:487
  19.1 24.9 %all-to-all-start = ((bf16[128,8,256]{2,1,0:T(8,128)(2,1)}), bf16[128,8,256]{2,1,0:T(8,128)(2,1)}, u32[]{:S(2)}, u32[]{:S(2)}) async-start(bf16[128,8,256]{2,1,0:T(8,128)(2,1)} %bitcast.7), calls=%async_computation | async-start | bytes 1048576 | tf_op jit(solution)/shard_map/all_to_all | solution.py:524
  28.7 13.0 %collective-permute-start.8 = (bf16[5,128,256]{2,1,0:T(8,128)(2,1)}, bf16[5,128,256]{2,1,0:T(8,128)(2,1)}, u32[]{:S(2)}, u32[]{:S(2)}) collective-permute-start(bf16[5,128,256]{2,1,0:T(8,128)(2,1)} %pad_maximum_fusion.refs_3_), channel_id=1, source_target_pairs={{0,4},{1,65},{2,6},{3,67},{4,0},{5,69},{6,2},{7,71},{8,12},{9,73},... | collective-permute-start | bytes 983048 | tf_op jit(solution)/shard_map/ppermute | solution.py:487
  31.1 11.1 %collective-permute-start.7 = (bf16[5,128,256]{2,1,0:T(8,128)(2,1)}, bf16[5,128,256]{2,1,0:T(8,128)(2,1)}, u32[]{:S(2)}, u32[]{:S(2)}) collective-permute-start(bf16[5,128,256]{2,1,0:T(8,128)(2,1)} %pad_maximum_fusion.refs_3_), channel_id=1, source_target_pairs={{0,6},{1,97},{2,0},{3,99},{4,2},{5,101},{6,4},{7,103},{8,14},{9,10... | collective-permute-start | bytes 983048 | tf_op jit(solution)/shard_map/ppermute | solution.py:487
  32.3 10.4 %collective-permute-start.6 = (bf16[5,128,256]{2,1,0:T(8,128)(2,1)}, bf16[5,128,256]{2,1,0:T(8,128)(2,1)}, u32[]{:S(2)}, u32[]{:S(2)}) collective-permute-start(bf16[5,128,256]{2,1,0:T(8,128)(2,1)} %pad_maximum_fusion.refs_3_), channel_id=1, source_target_pairs={{0,2},{1,33},{2,4},{3,35},{4,6},{5,37},{6,0},{7,39},{8,10},{9,41},... | collective-permute-start | bytes 983048 | tf_op jit(solution)/shard_map/ppermute | solution.py:487
  41.6 28.3 %collective-permute-start.9 = (bf16[5,128,256]{2,1,0:T(8,128)(2,1)}, bf16[5,128,256]{2,1,0:T(8,128)(2,1)}, u32[]{:S(2)}, u32[]{:S(2)}) collective-permute-start(bf16[5,128,256]{2,1,0:T(8,128)(2,1)} %pad_maximum_fusion.refs_3_), channel_id=1, source_target_pairs={{0,1},{1,0},{2,3},{3,2},{4,5},{5,4},{6,7},{7,6},{8,9},{9,8},{10,11... | collective-permute-start | bytes 983048 | tf_op jit(solution)/shard_map/ppermute | solution.py:500
  41.7 28.2 %collective-permute-start.12 = (bf16[5,128,256]{2,1,0:T(8,128)(2,1)}, bf16[5,128,256]{2,1,0:T(8,128)(2,1)}, u32[]{:S(2)}, u32[]{:S(2)}) collective-permute-start(bf16[5,128,256]{2,1,0:T(8,128)(2,1)} %collective-permute-done.8.refs_6_), channel_id=1, source_target_pairs={{0,1},{1,0},{2,3},{3,2},{4,5},{5,4},{6,7},{7,6},{8,9},{9,8},{10,11... | collective-permute-start | bytes 983048 | tf_op jit(solution)/shard_map/ppermute | solution.py:500
  42.2 27.7 %collective-permute-start.11 = (bf16[5,128,256]{2,1,0:T(8,128)(2,1)}, bf16[5,128,256]{2,1,0:T(8,128)(2,1)}, u32[]{:S(2)}, u32[]{:S(2)}) collective-permute-start(bf16[5,128,256]{2,1,0:T(8,128)(2,1)} %collective-permute-done.7.refs_5_), channel_id=1, source_target_pairs={{0,1},{1,0},{2,3},{3,2},{4,5},{5,4},{6,7},{7,6},{8,9},{9,8},{10,11... | collective-permute-start | bytes 983048 | tf_op jit(solution)/shard_map/ppermute | solution.py:500
  42.7 27.3 %collective-permute-start.10 = (bf16[5,128,256]{2,1,0:T(8,128)(2,1)}, bf16[5,128,256]{2,1,0:T(8,128)(2,1)}, u32[]{:S(2)}, u32[]{:S(2)}) collective-permute-start(bf16[5,128,256]{2,1,0:T(8,128)(2,1)} %collective-permute-done.6.refs_4_), channel_id=1, source_target_pairs={{0,1},{1,0},{2,3},{3,2},{4,5},{5,4},{6,7},{7,6},{8,9},{9,8},{10,11... | collective-permute-start | bytes 983048 | tf_op jit(solution)/shard_map/ppermute | solution.py:500

commit v2 on v1

--- a/solution.py
+++ b/solution.py
@@ -190,11 +190,11 @@
             all_hbm.at[pl.ds(block * n, n), :], target.at[:, pl.ds(j * 256, 256)], sems.at[sem]
         )
 
+    get_got.wait()
     get_count = [get_block(12 + j, count_ref, j, 8 + j) for j in range(4)]
     gets = [get_block(8 + j, query_ref, j, 2 + j) for j in range(2)]
     gets += [get_block(10 + j, value_ref, j, 4 + j) for j in range(2)]
     gets.append(start_copy(own_hbm, own_ref, sems.at[6]))
-    get_got.wait()
     got = got_ref[...]
     absent = got.astype(F32) > 1024.0
     rows = jnp.where(absent, 0.0, got.astype(F32)).astype(BF16)
@@ -345,16 +345,14 @@
             for head in range(HEADS):
                 shift_ref[pl.ds(head * n, n), :] = jnp.broadcast_to(own_ref[:, head : head + 1], (n, 128))
             get_lifted.wait()
-            for disk in range(disks):
-
-                @pl.when(seen(disk))
-                def _():
-                    for copy in token_copies(disk):
-                        copy.wait()
 
         def add_disk(disk, carry):
             @pl.when(seen(disk))
             def _():
+                if first:
+                    for copy in token_copies(disk):
+                        copy.wait()
+
                 def body(i, inner):
                     for u in range(unroll):
                         at = pl.ds(pl.multiple_of((i * unroll + u) * step, step), step)
@@ -377,7 +375,7 @@
 
         lax.fori_loop(0, disks, add_disk, 0)
 
-    add_disks(256, 8, True)
+    add_disks(512, 8, True)
 
     worst = jnp.max(jnp.max(den_ref[...], axis=0, keepdims=True))
 
@@ -488,12 +486,31 @@
     return got
 
 
+def planes():
+    groups = []
+    for core in range(2):
+        for fixed in range(4):
+            group = []
+            for a in range(4):
+                for b in range(4):
+                    at = (a, b, fixed) if core == 0 else (fixed, a, b)
+                    group.append(device_at(*at, core))
+            groups.append(group)
+    return groups
+
+
 def gather_tokens(disk_tokens):
     block = jnp.transpose(disk_tokens, (1, 0, 2))
-    block = jnp.concatenate([block] + spread(block, 0, 1), axis=1)
-    block = lax.optimization_barrier(block)
-    block = jnp.concatenate([block] + spread(block, 1, 2), axis=1)
-    block = lax.optimization_barrier(block)
+    disks, size, width = block.shape
+    block = lax.all_to_all(
+        jnp.broadcast_to(block, (16, disks, size, width)),
+        AXES,
+        split_axis=0,
+        concat_axis=0,
+        tiled=True,
+        axis_index_groups=planes(),
+    )
+    block = jnp.transpose(block, (1, 0, 2, 3)).reshape(disks, 16 * size, width)
     pieces = [block] + spread(block, 2, 0)
     swapped = []
     for piece in pieces:

time: 101 us -> 99.4 us (0.984)
  starting transfers between devices: 25.9 us -> 21.4 us
  waiting for transfers between devices: 3.92 us -> 7.74 us
  local copies, waits for them, and re-layouts: 0 us -> 3.2 us
  other arithmetic: 3.13 us -> 0 us
  Pallas kernels: 67.9 us -> 66.3 us
    ppermute x9 -> x3, starting transfers between devices: 15.7 us -> 4.42 us  [spread(): got.append(lax.ppermute(block, AXES, ring((first, by), (second, by))))]
    all_to_all x0 -> x1, starting transfers between devices: none -> 8.2 us  [gather_tokens(): lax.all_to_all(jnp.broadcast_to(block, (16, disks, size, width)), AXES, s...]
    all_to_all x0 -> x1, waiting for transfers between devices: none -> 7.72 us  [gather_tokens(): lax.all_to_all(jnp.broadcast_to(block, (16, disks, size, width)), AXES, s...]
    ppermute x9 -> x3, waiting for transfers between devices: 3.91 us -> 0.01 us  [spread(): got.append(lax.ppermute(block, AXES, ring((first, by), (second, by))))]
    concatenate x2 -> x0, other arithmetic: 3.13 us -> none  [the longest x1 1.76 us: gather_tokens(): block = jnp.concatenate([block] + spread(block, 1, 2), axis=1)]
    pallas_call x1, Pallas kernels: 31 us -> 29.1 us  [disk_attend(): pl.pallas_call(functools.partial(disk_kernel, pieces=len(pieces)), out_sh...]
    reshape x0 -> x1, local copies, waits for them, and re-layouts: none -> 1.74 us  [gather_tokens(): block = jnp.transpose(block, (1, 0, 2, 3)).reshape(disks, 16 * size, width)]
    all_to_all x1, starting transfers between devices: 7.8 us -> 6.14 us  [local(): lax.all_to_all(send.reshape(devices, 8, width), AXES, split_axis=0, conca...]
  transfers between devices with their start and end apart: 14 -> 9, of which waited for: 2 -> 1; matrix products, arithmetic and copies ran while one was open for 2% -> 2% of each run, Pallas kernels for 36% -> 38%
where the time goes in v2:
time: 99.4 us; the launch traced here: 98.9 us
  Pallas kernels  66.3 us (67%)
  starting transfers between devices  21.4 us (22%)
  waiting for transfers between devices  7.74 us (8%)
  local copies, waits for them, and re-layouts  3.2 us (3%)
    pallas_call x1, Pallas kernels, disk_attend(): pl.pallas_call(functools.partial(disk_kernel, pieces=len(pieces)), out_sh...  29.1 us
    pallas_call x1, Pallas kernels, near_attend(): pl.pallas_call(near_kernel, out_shape=tuple((shape(*o) for o in outs)), i...  26.1 us
    pallas_call x1, Pallas kernels, prep(): pl.pallas_call(prep_kernel, out_shape=tuple((shape(*o) for o in outs)), i...  8.46 us
    all_to_all x1, starting transfers between devices, gather_tokens(): lax.all_to_all(jnp.broadcast_to(block, (16, disks, size, width)), AXES, s...  8.2 us
    all_to_all x1, waiting for transfers between devices, gather_tokens(): lax.all_to_all(jnp.broadcast_to(block, (16, disks, size, width)), AXES, s...  7.72 us
    all_to_all x1, starting transfers between devices, local(): lax.all_to_all(send.reshape(devices, 8, width), AXES, split_axis=0, conca...  6.14 us
    ppermute x3, starting transfers between devices, spread(): got.append(lax.ppermute(block, AXES, ring((first, by), (second, by))))  4.42 us
    pallas_call x1, Pallas kernels, place(): pl.pallas_call(place_kernel, out_shape=shape((slots, rows.shape[1]), BF16...  2.64 us
  transfers between devices with their start and end apart: 9, of which 1 were waited for; matrix products, arithmetic and copies ran while one was open for 2% of the time, Pallas kernels for 38%

profile of v2, /device:TPU:0, one launch (start us, length us, event | category | flops | bytes accessed | tf_op | source)
XLA Modules:
  0.0 98.9 jit_solution(15161819868496200038)
XLA Ops:
  0.0 1.5 %broadcast_in_dim.3 = bf16[16,5,8,256]{3,2,1,0:T(8,128)(2,1)} broadcast(bf16[5,8,256]{2,1,0:T(8,128)(2,1)} %bitcast.13), dimensions={1,2,3} | broadcast | bytes 348160 | tf_op jit(solution)/shard_map/broadcast_in_dim | solution.py:506
  1.5 8.2 %all-to-all-start = ((bf16[16,5,8,256]{3,2,1,0:T(8,128)(2,1)}), bf16[16,5,8,256]{3,2,1,0:T(8,128)(2,1)}, u32[]{:S(2)}, u32[]{:S(2)}) async-start(bf16[16,5,8,256]{3,2,1,0:T(8,128)(2,1)} %broadcast_in_dim.3), calls=%async_computation | async-start | bytes 655360 | tf_op jit(solution)/shard_map/all_to_all | solution.py:505
  9.7 2.6 %place.1 = bf16[1024,256]{1,0:T(8,128)(2,1)} custom-call(s32[1,512]{1,0:T(1,128)} %bitcast.16, bf16[512,256]{1,0:T(8,128)(2,1)} %rows_ref.1), custom_call_target="tpu_custom_call" | custom-call | flops 1000000000 | bytes 1000000 | tf_op jit(solution)/shard_map/place/pallas_call | solution.py:71
  12.3 7.7 %all-to-all-done = bf16[16,5,8,256]{3,2,1,0:T(8,128)(2,1)} async-done(((bf16[16,5,8,256]{3,2,1,0:T(8,128)(2,1)}), bf16[16,5,8,256]{3,2,1,0:T(8,128)(2,1)}, u32[]{:S(2)}, u32[]{:S(2)}) %all-to-all-start) | async-done | bytes 327712 | tf_op jit(solution)/shard_map/all_to_all | solution.py:505
  20.0 6.1 %all-to-all-start.1 = ((bf16[128,8,256]{2,1,0:T(8,128)(2,1)}), bf16[128,8,256]{2,1,0:T(8,128)(2,1)}, u32[]{:S(2)}, u32[]{:S(2)}) async-start(bf16[128,8,256]{2,1,0:T(8,128)(2,1)} %bitcast.12), calls=%async_computation.1 | async-start | bytes 1048576 | tf_op jit(solution)/shard_map/all_to_all | solution.py:541
  26.2 1.7 %copy_bitcast_fusion.refs_3_ = bf16[5,128,256]{2,1,0:T(8,128)(2,1)} fusion(bf16[16,5,8,256]{3,2,1,0:T(8,128)(2,1)} %all-to-all-done), kind=kLoop, calls=%fused_computation | loop fusion | bytes 655360 | tf_op jit(solution)/shard_map/reshape | solution.py:513
  27.9 0.9 collective-permute-start
  28.8 2.4 %collective-permute-start.1 = (bf16[5,128,256]{2,1,0:T(8,128)(2,1)}, bf16[5,128,256]{2,1,0:T(8,128)(2,1)}, u32[]{:S(2)}, u32[]{:S(2)}) collective-permute-start(bf16[5,128,256]{2,1,0:T(8,128)(2,1)} %copy_bitcast_fusion.refs_3_), channel_id=1, source_target_pairs={{0,6},{1,97},{2,0},{3,99},{4,2},{5,101},{6,4},{7,103},{8,14},{9,10... | collective-permute-start | bytes 983048 | tf_op jit(solution)/shard_map/ppermute | solution.py:485
  31.2 1.2 %collective-permute-start.2 = (bf16[5,128,256]{2,1,0:T(8,128)(2,1)}, bf16[5,128,256]{2,1,0:T(8,128)(2,1)}, u32[]{:S(2)}, u32[]{:S(2)}) collective-permute-start(bf16[5,128,256]{2,1,0:T(8,128)(2,1)} %copy_bitcast_fusion.refs_3_), channel_id=1, source_target_pairs={{0,4},{1,65},{2,6},{3,67},{4,0},{5,69},{6,2},{7,71},{8,12},{9,73},... | collective-permute-start | bytes 983048 | tf_op jit(solution)/shard_map/ppermute | solution.py:485
  32.4 8.5 %prep.1 = (bf16[8192,256]{1,0:T(8,128)(2,1)}, f32[512,128]{1,0:T(8,128)}) custom-call(s32[32,512]{1,0:T(8,128)} %bitcast.14, s32[32,512]{1,0:T(8,128)} %bitcast.15, bf16[512,512]{1,0:T(8,128)(2,1)} %refs_17_.1, f32[1,512]{1,0:T(1,128)} %bitcast.17, bf16[512,512]{1,0:T(8,128)(2,1)} %wq_hbm.1, bf16[512,1024]{1,0:T(8,128)(2,1)} %wkv_hbm.1, ...), custom_call_target="tpu_custom_call" | custom-call | flops 8000000000 | bytes 8000000 | tf_op jit(solution)/shard_map/prep/pallas_call | solution.py:161
  40.8 0.1 collective-permute-start.3
  40.9 0.0 collective-permute-done.refs_4_
  40.9 0.5 collective-permute-start.4
  41.4 0.0 collective-permute-done.1.refs_5_
  41.4 0.1 collective-permute-start.5
  41.5 0.0 collective-permute-done.2.refs_6_
  41.5 1.9 %collective-permute-start.6 = (bf16[5,128,256]{2,1,0:T(8,128)(2,1)}, bf16[5,128,256]{2,1,0:T(8,128)(2,1)}, u32[]{:S(2)}, u32[]{:S(2)}) collective-permute-start(bf16[5,128,256]{2,1,0:T(8,128)(2,1)} %collective-permute-done.2.refs_6_), channel_id=1, source_target_pairs={{0,1},{1,0},{2,3},{3,2},{4,5},{5,4},{6,7},{7,6},{8,9},{9,8},{10,11... | collective-permute-start | bytes 983048 | tf_op jit(solution)/shard_map/ppermute | solution.py:517
  43.5 0.0 all-to-all-done.1
  43.5 26.1 %near_attend.1 = (f32[512,128]{1,0:T(8,128)}, f32[512,128]{1,0:T(8,128)}, f32[512,512]{1,0:T(8,128)}) custom-call(bf16[1024,256]{1,0:T(8,128)(2,1)} %bitcast.8.got_hbm, bf16[256,1024]{1,0:T(8,128)(2,1)} %w_hbm.1, bf16[8192,256]{1,0:T(8,128)(2,1)} %get-tuple-element.10.all_hbm.refs_2_, f32[512,128]{1,0:T(8,128)} %get-tuple-element.11.own_hbm.refs_11_), custom_call_target="tpu_custom_call" | custom-call | flops 5000000000 | bytes 5000000 | tf_op jit(solution)/shard_map/near_attend/pallas_call | solution.py:280
  69.6 0.0 collective-permute-done.3.refs_7_
  69.6 0.0 collective-permute-done.4.refs_8_
  69.6 0.0 collective-permute-done.5.refs_9_
  69.7 0.0 collective-permute-done.6.refs_10_
  69.7 29.1 %disk_attend.1 = bf16[512,512]{1,0:T(8,128)(2,1)} custom-call(s32[5]{0:T(128)} %refs_0_.1, s32[5]{0:T(128)} %refs_1_.1, bf16[8192,256]{1,0:T(8,128)(2,1)} %get-tuple-element.10.all_hbm.refs_2_, bf16[5,128,256]{2,1,0:T(8,128)(2,1)} %copy_bitcast_fusion.refs_3_, bf16[5,128,256]{2,1,0:T(8,128)(2,1)} %collective-permute-done.refs_4_, ...), custom_call_target="tpu_custom_call" | custom-call | flops 16000000000 | bytes 10000000 | tf_op jit(solution)/shard_map/disk_attend/pallas_call | solution.py:436
Async XLA Ops:
  1.5 18.6 %all-to-all-start = ((bf16[16,5,8,256]{3,2,1,0:T(8,128)(2,1)}), bf16[16,5,8,256]{3,2,1,0:T(8,128)(2,1)}, u32[]{:S(2)}, u32[]{:S(2)}) async-start(bf16[16,5,8,256]{3,2,1,0:T(8,128)(2,1)} %broadcast_in_dim.3), calls=%async_computation | async-start | bytes 655360 | tf_op jit(solution)/shard_map/all_to_all | solution.py:505
  20.0 23.4 %all-to-all-start.1 = ((bf16[128,8,256]{2,1,0:T(8,128)(2,1)}), bf16[128,8,256]{2,1,0:T(8,128)(2,1)}, u32[]{:S(2)}, u32[]{:S(2)}) async-start(bf16[128,8,256]{2,1,0:T(8,128)(2,1)} %bitcast.12), calls=%async_computation.1 | async-start | bytes 1048576 | tf_op jit(solution)/shard_map/all_to_all | solution.py:541
  27.9 13.0 %collective-permute-start = (bf16[5,128,256]{2,1,0:T(8,128)(2,1)}, bf16[5,128,256]{2,1,0:T(8,128)(2,1)}, u32[]{:S(2)}, u32[]{:S(2)}) collective-permute-start(bf16[5,128,256]{2,1,0:T(8,128)(2,1)} %copy_bitcast_fusion.refs_3_), channel_id=1, source_target_pairs={{0,2},{1,33},{2,4},{3,35},{4,6},{5,37},{6,0},{7,39},{8,10},{9,41},... | collective-permute-start | bytes 983048 | tf_op jit(solution)/shard_map/ppermute | solution.py:485
  28.8 12.6 %collective-permute-start.1 = (bf16[5,128,256]{2,1,0:T(8,128)(2,1)}, bf16[5,128,256]{2,1,0:T(8,128)(2,1)}, u32[]{:S(2)}, u32[]{:S(2)}) collective-permute-start(bf16[5,128,256]{2,1,0:T(8,128)(2,1)} %copy_bitcast_fusion.refs_3_), channel_id=1, source_target_pairs={{0,6},{1,97},{2,0},{3,99},{4,2},{5,101},{6,4},{7,103},{8,14},{9,10... | collective-permute-start | bytes 983048 | tf_op jit(solution)/shard_map/ppermute | solution.py:485
  31.2 10.4 %collective-permute-start.2 = (bf16[5,128,256]{2,1,0:T(8,128)(2,1)}, bf16[5,128,256]{2,1,0:T(8,128)(2,1)}, u32[]{:S(2)}, u32[]{:S(2)}) collective-permute-start(bf16[5,128,256]{2,1,0:T(8,128)(2,1)} %copy_bitcast_fusion.refs_3_), channel_id=1, source_target_pairs={{0,4},{1,65},{2,6},{3,67},{4,0},{5,69},{6,2},{7,71},{8,12},{9,73},... | collective-permute-start | bytes 983048 | tf_op jit(solution)/shard_map/ppermute | solution.py:485
  40.8 28.8 %collective-permute-start.3 = (bf16[5,128,256]{2,1,0:T(8,128)(2,1)}, bf16[5,128,256]{2,1,0:T(8,128)(2,1)}, u32[]{:S(2)}, u32[]{:S(2)}) collective-permute-start(bf16[5,128,256]{2,1,0:T(8,128)(2,1)} %copy_bitcast_fusion.refs_3_), channel_id=1, source_target_pairs={{0,1},{1,0},{2,3},{3,2},{4,5},{5,4},{6,7},{7,6},{8,9},{9,8},{10,11... | collective-permute-start | bytes 983048 | tf_op jit(solution)/shard_map/ppermute | solution.py:517
  40.9 28.7 %collective-permute-start.4 = (bf16[5,128,256]{2,1,0:T(8,128)(2,1)}, bf16[5,128,256]{2,1,0:T(8,128)(2,1)}, u32[]{:S(2)}, u32[]{:S(2)}) collective-permute-start(bf16[5,128,256]{2,1,0:T(8,128)(2,1)} %collective-permute-done.refs_4_), channel_id=1, source_target_pairs={{0,1},{1,0},{2,3},{3,2},{4,5},{5,4},{6,7},{7,6},{8,9},{9,8},{10,11... | collective-permute-start | bytes 983048 | tf_op jit(solution)/shard_map/ppermute | solution.py:517
  41.4 28.2 %collective-permute-start.5 = (bf16[5,128,256]{2,1,0:T(8,128)(2,1)}, bf16[5,128,256]{2,1,0:T(8,128)(2,1)}, u32[]{:S(2)}, u32[]{:S(2)}) collective-permute-start(bf16[5,128,256]{2,1,0:T(8,128)(2,1)} %collective-permute-done.1.refs_5_), channel_id=1, source_target_pairs={{0,1},{1,0},{2,3},{3,2},{4,5},{5,4},{6,7},{7,6},{8,9},{9,8},{10,11... | collective-permute-start | bytes 983048 | tf_op jit(solution)/shard_map/ppermute | solution.py:517
  41.5 28.1 %collective-permute-start.6 = (bf16[5,128,256]{2,1,0:T(8,128)(2,1)}, bf16[5,128,256]{2,1,0:T(8,128)(2,1)}, u32[]{:S(2)}, u32[]{:S(2)}) collective-permute-start(bf16[5,128,256]{2,1,0:T(8,128)(2,1)} %collective-permute-done.2.refs_6_), channel_id=1, source_target_pairs={{0,1},{1,0},{2,3},{3,2},{4,5},{5,4},{6,7},{7,6},{8,9},{9,8},{10,11... | collective-permute-start | bytes 983048 | tf_op jit(solution)/shard_map/ppermute | solution.py:517

commit v3 on v1

--- a/solution.py
+++ b/solution.py
@@ -190,11 +190,11 @@
             all_hbm.at[pl.ds(block * n, n), :], target.at[:, pl.ds(j * 256, 256)], sems.at[sem]
         )
 
+    get_got.wait()
     get_count = [get_block(12 + j, count_ref, j, 8 + j) for j in range(4)]
     gets = [get_block(8 + j, query_ref, j, 2 + j) for j in range(2)]
     gets += [get_block(10 + j, value_ref, j, 4 + j) for j in range(2)]
     gets.append(start_copy(own_hbm, own_ref, sems.at[6]))
-    get_got.wait()
     got = got_ref[...]
     absent = got.astype(F32) > 1024.0
     rows = jnp.where(absent, 0.0, got.astype(F32)).astype(BF16)
@@ -345,16 +345,14 @@
             for head in range(HEADS):
                 shift_ref[pl.ds(head * n, n), :] = jnp.broadcast_to(own_ref[:, head : head + 1], (n, 128))
             get_lifted.wait()
-            for disk in range(disks):
-
-                @pl.when(seen(disk))
-                def _():
-                    for copy in token_copies(disk):
-                        copy.wait()
 
         def add_disk(disk, carry):
             @pl.when(seen(disk))
             def _():
+                if first:
+                    for copy in token_copies(disk):
+                        copy.wait()
+
                 def body(i, inner):
                     for u in range(unroll):
                         at = pl.ds(pl.multiple_of((i * unroll + u) * step, step), step)
@@ -377,7 +375,7 @@
 
         lax.fori_loop(0, disks, add_disk, 0)
 
-    add_disks(256, 8, True)
+    add_disks(512, 8, True)
 
     worst = jnp.max(jnp.max(den_ref[...], axis=0, keepdims=True))
 

time: 101 us -> 99.7 us (0.987)
  Pallas kernels: 67.9 us -> 66.1 us
    pallas_call x1, Pallas kernels: 31 us -> 29.1 us  [disk_attend(): pl.pallas_call(functools.partial(disk_kernel, pieces=len(pieces)), out_sh...]
  transfers between devices with their start and end apart: 14 -> 14, of which waited for: 2 -> 2; matrix products, arithmetic and copies ran while one was open for 2% -> 2% of each run, Pallas kernels for 36% -> 37%
where the time goes in v3:
time: 99.7 us; the launch traced here: 99.3 us
  Pallas kernels  66.1 us (66%)
  starting transfers between devices  25.9 us (26%)
  waiting for transfers between devices  3.92 us (4%)
  other arithmetic  3.13 us (3%)
    pallas_call x1, Pallas kernels, disk_attend(): pl.pallas_call(functools.partial(disk_kernel, pieces=len(pieces)), out_sh...  29.1 us
    pallas_call x1, Pallas kernels, near_attend(): pl.pallas_call(near_kernel, out_shape=tuple((shape(*o) for o in outs)), i...  25.9 us
    ppermute x9, starting transfers between devices, spread(): got.append(lax.ppermute(block, AXES, ring((first, by), (second, by))))  15.7 us
    pallas_call x1, Pallas kernels, prep(): pl.pallas_call(prep_kernel, out_shape=tuple((shape(*o) for o in outs)), i...  8.44 us
    all_to_all x1, starting transfers between devices, local(): lax.all_to_all(send.reshape(devices, 8, width), AXES, split_axis=0, conca...  7.8 us
    ppermute x9, waiting for transfers between devices, spread(): got.append(lax.ppermute(block, AXES, ring((first, by), (second, by))))  3.91 us
    pallas_call x1, Pallas kernels, place(): pl.pallas_call(place_kernel, out_shape=shape((slots, rows.shape[1]), BF16...  2.64 us
    ppermute x4, starting transfers between devices, gather_tokens(): swapped.append(lax.ppermute(piece, AXES, other_core()))  2.42 us
  transfers between devices with their start and end apart: 14, of which 2 were waited for; matrix products, arithmetic and copies ran while one was open for 2% of the time, Pallas kernels for 37%

profile of v3, /device:TPU:0, one launch (start us, length us, event | category | flops | bytes accessed | tf_op | source)
XLA Modules:
  0.0 99.3 jit_solution(3523614624514186275)
XLA Ops:
  0.0 4.0 %collective-permute-start.2 = (bf16[5,8,256]{2,1,0:T(8,128)(2,1)}, bf16[5,8,256]{2,1,0:T(8,128)(2,1)S(1)}, u32[]{:S(2)}, u32[]{:S(2)}) collective-permute-start(bf16[5,8,256]{2,1,0:T(8,128)(2,1)} %bitcast.8), channel_id=1, source_target_pairs={{0,64},{1,17},{2,66},{3,19},{4,68},{5,21},{6,70},{7,23},{8,72},{9,... | collective-permute-start | bytes 61448 | tf_op jit(solution)/shard_map/ppermute | solution.py:485
  4.0 0.7 collective-permute-start.1
  4.7 1.3 %collective-permute-start = (bf16[5,8,256]{2,1,0:T(8,128)(2,1)}, bf16[5,8,256]{2,1,0:T(8,128)(2,1)S(1)}, u32[]{:S(2)}, u32[]{:S(2)}) collective-permute-start(bf16[5,8,256]{2,1,0:T(8,128)(2,1)} %bitcast.10), channel_id=1, source_target_pairs={{0,32},{1,9},{2,34},{3,11},{4,36},{5,13},{6,38},{7,15},{8,40},{9,1... | collective-permute-start | bytes 61448 | tf_op jit(solution)/shard_map/ppermute | solution.py:485
  6.0 0.0 collective-permute-done.2
  6.0 2.0 %collective-permute-done.1 = bf16[5,8,256]{2,1,0:T(8,128)(2,1)S(1)} collective-permute-done((bf16[5,8,256]{2,1,0:T(8,128)(2,1)}, bf16[5,8,256]{2,1,0:T(8,128)(2,1)S(1)}, u32[]{:S(2)}, u32[]{:S(2)}) %collective-permute-start.1) | collective-permute-done | bytes 20512 | tf_op jit(solution)/shard_map/ppermute | solution.py:485
  8.0 1.9 %collective-permute-done = bf16[5,8,256]{2,1,0:T(8,128)(2,1)S(1)} collective-permute-done((bf16[5,8,256]{2,1,0:T(8,128)(2,1)}, bf16[5,8,256]{2,1,0:T(8,128)(2,1)S(1)}, u32[]{:S(2)}, u32[]{:S(2)}) %collective-permute-start) | collective-permute-done | bytes 20512 | tf_op jit(solution)/shard_map/ppermute | solution.py:485
  9.9 1.4 %pad_maximum_fusion.1 = bf16[5,32,256]{2,1,0:T(8,128)(2,1)} fusion(bf16[5,8,256]{2,1,0:T(8,128)(2,1)S(1)} %collective-permute-done.2, bf16[5,8,256]{2,1,0:T(8,128)(2,1)S(1)} %collective-permute-done.1, bf16[5,8,256]{2,1,0:T(8,128)(2,1)S(1)} %collective-permute-done, bf16[5,8,256]{2,1,0:T(8,128)(2,1)} %bitcast.11), kind=kLoop, calls=%fused_computation.1 | loop fusion | flops 327680 | bytes 163840 | tf_op jit(solution)/shard_map/concatenate | solution.py:491
  11.3 3.2 %collective-permute-start.5 = (bf16[5,32,256]{2,1,0:T(8,128)(2,1)}, bf16[5,32,256]{2,1,0:T(8,128)(2,1)}, u32[]{:S(2)}, u32[]{:S(2)}) collective-permute-start(bf16[5,32,256]{2,1,0:T(8,128)(2,1)} %pad_maximum_fusion.1), channel_id=1, source_target_pairs={{0,16},{1,5},{2,18},{3,7},{4,20},{5,1},{6,22},{7,3},{8,24},{9,13},... | collective-permute-start | bytes 245768 | tf_op jit(solution)/shard_map/ppermute | solution.py:485
  14.5 1.1 %collective-permute-start.4 = (bf16[5,32,256]{2,1,0:T(8,128)(2,1)}, bf16[5,32,256]{2,1,0:T(8,128)(2,1)}, u32[]{:S(2)}, u32[]{:S(2)}) collective-permute-start(bf16[5,32,256]{2,1,0:T(8,128)(2,1)} %pad_maximum_fusion.1), channel_id=1, source_target_pairs={{0,24},{1,7},{2,26},{3,1},{4,28},{5,3},{6,30},{7,5},{8,0},{9,15},{... | collective-permute-start | bytes 245768 | tf_op jit(solution)/shard_map/ppermute | solution.py:485
  15.5 1.0 collective-permute-start.3
  16.5 2.6 %place.1 = bf16[1024,256]{1,0:T(8,128)(2,1)} custom-call(s32[1,512]{1,0:T(1,128)} %bitcast.14, bf16[512,256]{1,0:T(8,128)(2,1)} %rows_ref.1), custom_call_target="tpu_custom_call" | custom-call | flops 1000000000 | bytes 1000000 | tf_op jit(solution)/shard_map/place/pallas_call | solution.py:71
  19.1 7.8 %all-to-all-start = ((bf16[128,8,256]{2,1,0:T(8,128)(2,1)}), bf16[128,8,256]{2,1,0:T(8,128)(2,1)}, u32[]{:S(2)}, u32[]{:S(2)}) async-start(bf16[128,8,256]{2,1,0:T(8,128)(2,1)} %bitcast.7), calls=%async_computation | async-start | bytes 1048576 | tf_op jit(solution)/shard_map/all_to_all | solution.py:522
  27.0 0.0 collective-permute-done.5
  27.0 1.8 %pad_maximum_fusion.refs_3_ = bf16[5,128,256]{2,1,0:T(8,128)(2,1)} fusion(bf16[5,32,256]{2,1,0:T(8,128)(2,1)} %collective-permute-done.5, bf16[5,32,256]{2,1,0:T(8,128)(2,1)} %collective-permute-done.4, bf16[5,32,256]{2,1,0:T(8,128)(2,1)} %collective-permute-done.3, bf16[5,32,256]{2,1,0:T(8,128)(2,1)} %pad_maximum_fusion.1), kind=kLoop, calls=%fused_computation | loop fusion | flops 1310720 | bytes 655360 | tf_op jit(solution)/shard_map/concatenate | solution.py:493
  28.7 2.4 %collective-permute-start.8 = (bf16[5,128,256]{2,1,0:T(8,128)(2,1)}, bf16[5,128,256]{2,1,0:T(8,128)(2,1)}, u32[]{:S(2)}, u32[]{:S(2)}) collective-permute-start(bf16[5,128,256]{2,1,0:T(8,128)(2,1)} %pad_maximum_fusion.refs_3_), channel_id=1, source_target_pairs={{0,4},{1,65},{2,6},{3,67},{4,0},{5,69},{6,2},{7,71},{8,12},{9,73},... | collective-permute-start | bytes 983048 | tf_op jit(solution)/shard_map/ppermute | solution.py:485
  31.1 1.2 %collective-permute-start.7 = (bf16[5,128,256]{2,1,0:T(8,128)(2,1)}, bf16[5,128,256]{2,1,0:T(8,128)(2,1)}, u32[]{:S(2)}, u32[]{:S(2)}) collective-permute-start(bf16[5,128,256]{2,1,0:T(8,128)(2,1)} %pad_maximum_fusion.refs_3_), channel_id=1, source_target_pairs={{0,6},{1,97},{2,0},{3,99},{4,2},{5,101},{6,4},{7,103},{8,14},{9,10... | collective-permute-start | bytes 983048 | tf_op jit(solution)/shard_map/ppermute | solution.py:485
  32.3 0.9 collective-permute-start.6
  33.2 8.4 %prep.1 = (bf16[8192,256]{1,0:T(8,128)(2,1)}, f32[512,128]{1,0:T(8,128)}) custom-call(s32[32,512]{1,0:T(8,128)} %bitcast.12, s32[32,512]{1,0:T(8,128)} %bitcast.13, bf16[512,512]{1,0:T(8,128)(2,1)} %refs_17_.1, f32[1,512]{1,0:T(1,128)} %bitcast.15, bf16[512,512]{1,0:T(8,128)(2,1)} %wq_hbm.1, bf16[512,1024]{1,0:T(8,128)(2,1)} %wkv_hbm.1, ...), custom_call_target="tpu_custom_call" | custom-call | flops 8000000000 | bytes 8000000 | tf_op jit(solution)/shard_map/prep/pallas_call | solution.py:161
  41.6 0.1 collective-permute-start.9
  41.7 0.5 collective-permute-start.12
  42.2 0.4 collective-permute-start.11
  42.7 1.4 %collective-permute-start.10 = (bf16[5,128,256]{2,1,0:T(8,128)(2,1)}, bf16[5,128,256]{2,1,0:T(8,128)(2,1)}, u32[]{:S(2)}, u32[]{:S(2)}) collective-permute-start(bf16[5,128,256]{2,1,0:T(8,128)(2,1)} %collective-permute-done.6.refs_4_), channel_id=1, source_target_pairs={{0,1},{1,0},{2,3},{3,2},{4,5},{5,4},{6,7},{7,6},{8,9},{9,8},{10,11... | collective-permute-start | bytes 983048 | tf_op jit(solution)/shard_map/ppermute | solution.py:498
  44.1 25.9 %near_attend.1 = (f32[512,128]{1,0:T(8,128)}, f32[512,128]{1,0:T(8,128)}, f32[512,512]{1,0:T(8,128)}) custom-call(bf16[1024,256]{1,0:T(8,128)(2,1)} %bitcast.6.got_hbm, bf16[256,1024]{1,0:T(8,128)(2,1)} %w_hbm.1, bf16[8192,256]{1,0:T(8,128)(2,1)} %get-tuple-element.10.all_hbm.refs_2_, f32[512,128]{1,0:T(8,128)} %get-tuple-element.11.own_hbm.refs_11_), custom_call_target="tpu_custom_call" | custom-call | flops 5000000000 | bytes 5000000 | tf_op jit(solution)/shard_map/near_attend/pallas_call | solution.py:280
  70.1 29.1 %disk_attend.1 = bf16[512,512]{1,0:T(8,128)(2,1)} custom-call(s32[5]{0:T(128)} %refs_0_.1, s32[5]{0:T(128)} %refs_1_.1, bf16[8192,256]{1,0:T(8,128)(2,1)} %get-tuple-element.10.all_hbm.refs_2_, bf16[5,128,256]{2,1,0:T(8,128)(2,1)} %pad_maximum_fusion.refs_3_, bf16[5,128,256]{2,1,0:T(8,128)(2,1)} %collective-permute-done.6.refs_4_, ...), custom_call_target="tpu_custom_call" | custom-call | flops 16000000000 | bytes 10000000 | tf_op jit(solution)/shard_map/disk_attend/pallas_call | solution.py:436
  (10 shorter events, 0.0 us)
Async XLA Ops:
  0.0 6.0 %collective-permute-start.2 = (bf16[5,8,256]{2,1,0:T(8,128)(2,1)}, bf16[5,8,256]{2,1,0:T(8,128)(2,1)S(1)}, u32[]{:S(2)}, u32[]{:S(2)}) collective-permute-start(bf16[5,8,256]{2,1,0:T(8,128)(2,1)} %bitcast.8), channel_id=1, source_target_pairs={{0,64},{1,17},{2,66},{3,19},{4,68},{5,21},{6,70},{7,23},{8,72},{9,... | collective-permute-start | bytes 61448 | tf_op jit(solution)/shard_map/ppermute | solution.py:485
  4.0 4.0 %collective-permute-start.1 = (bf16[5,8,256]{2,1,0:T(8,128)(2,1)}, bf16[5,8,256]{2,1,0:T(8,128)(2,1)S(1)}, u32[]{:S(2)}, u32[]{:S(2)}) collective-permute-start(bf16[5,8,256]{2,1,0:T(8,128)(2,1)} %bitcast.9), channel_id=1, source_target_pairs={{0,96},{1,25},{2,98},{3,27},{4,100},{5,29},{6,102},{7,31},{8,104},... | collective-permute-start | bytes 61448 | tf_op jit(solution)/shard_map/ppermute | solution.py:485
  4.7 5.2 %collective-permute-start = (bf16[5,8,256]{2,1,0:T(8,128)(2,1)}, bf16[5,8,256]{2,1,0:T(8,128)(2,1)S(1)}, u32[]{:S(2)}, u32[]{:S(2)}) collective-permute-start(bf16[5,8,256]{2,1,0:T(8,128)(2,1)} %bitcast.10), channel_id=1, source_target_pairs={{0,32},{1,9},{2,34},{3,11},{4,36},{5,13},{6,38},{7,15},{8,40},{9,1... | collective-permute-start | bytes 61448 | tf_op jit(solution)/shard_map/ppermute | solution.py:485
  11.3 15.7 %collective-permute-start.5 = (bf16[5,32,256]{2,1,0:T(8,128)(2,1)}, bf16[5,32,256]{2,1,0:T(8,128)(2,1)}, u32[]{:S(2)}, u32[]{:S(2)}) collective-permute-start(bf16[5,32,256]{2,1,0:T(8,128)(2,1)} %pad_maximum_fusion.1), channel_id=1, source_target_pairs={{0,16},{1,5},{2,18},{3,7},{4,20},{5,1},{6,22},{7,3},{8,24},{9,13},... | collective-permute-start | bytes 245768 | tf_op jit(solution)/shard_map/ppermute | solution.py:485
  14.5 12.5 %collective-permute-start.4 = (bf16[5,32,256]{2,1,0:T(8,128)(2,1)}, bf16[5,32,256]{2,1,0:T(8,128)(2,1)}, u32[]{:S(2)}, u32[]{:S(2)}) collective-permute-start(bf16[5,32,256]{2,1,0:T(8,128)(2,1)} %pad_maximum_fusion.1), channel_id=1, source_target_pairs={{0,24},{1,7},{2,26},{3,1},{4,28},{5,3},{6,30},{7,5},{8,0},{9,15},{... | collective-permute-start | bytes 245768 | tf_op jit(solution)/shard_map/ppermute | solution.py:485
  15.5 11.4 %collective-permute-start.3 = (bf16[5,32,256]{2,1,0:T(8,128)(2,1)}, bf16[5,32,256]{2,1,0:T(8,128)(2,1)}, u32[]{:S(2)}, u32[]{:S(2)}) collective-permute-start(bf16[5,32,256]{2,1,0:T(8,128)(2,1)} %pad_maximum_fusion.1), channel_id=1, source_target_pairs={{0,8},{1,3},{2,10},{3,5},{4,12},{5,7},{6,14},{7,1},{8,16},{9,11},{... | collective-permute-start | bytes 245768 | tf_op jit(solution)/shard_map/ppermute | solution.py:485
  19.1 24.9 %all-to-all-start = ((bf16[128,8,256]{2,1,0:T(8,128)(2,1)}), bf16[128,8,256]{2,1,0:T(8,128)(2,1)}, u32[]{:S(2)}, u32[]{:S(2)}) async-start(bf16[128,8,256]{2,1,0:T(8,128)(2,1)} %bitcast.7), calls=%async_computation | async-start | bytes 1048576 | tf_op jit(solution)/shard_map/all_to_all | solution.py:522
  28.7 13.0 %collective-permute-start.8 = (bf16[5,128,256]{2,1,0:T(8,128)(2,1)}, bf16[5,128,256]{2,1,0:T(8,128)(2,1)}, u32[]{:S(2)}, u32[]{:S(2)}) collective-permute-start(bf16[5,128,256]{2,1,0:T(8,128)(2,1)} %pad_maximum_fusion.refs_3_), channel_id=1, source_target_pairs={{0,4},{1,65},{2,6},{3,67},{4,0},{5,69},{6,2},{7,71},{8,12},{9,73},... | collective-permute-start | bytes 983048 | tf_op jit(solution)/shard_map/ppermute | solution.py:485
  31.1 11.1 %collective-permute-start.7 = (bf16[5,128,256]{2,1,0:T(8,128)(2,1)}, bf16[5,128,256]{2,1,0:T(8,128)(2,1)}, u32[]{:S(2)}, u32[]{:S(2)}) collective-permute-start(bf16[5,128,256]{2,1,0:T(8,128)(2,1)} %pad_maximum_fusion.refs_3_), channel_id=1, source_target_pairs={{0,6},{1,97},{2,0},{3,99},{4,2},{5,101},{6,4},{7,103},{8,14},{9,10... | collective-permute-start | bytes 983048 | tf_op jit(solution)/shard_map/ppermute | solution.py:485
  32.3 10.4 %collective-permute-start.6 = (bf16[5,128,256]{2,1,0:T(8,128)(2,1)}, bf16[5,128,256]{2,1,0:T(8,128)(2,1)}, u32[]{:S(2)}, u32[]{:S(2)}) collective-permute-start(bf16[5,128,256]{2,1,0:T(8,128)(2,1)} %pad_maximum_fusion.refs_3_), channel_id=1, source_target_pairs={{0,2},{1,33},{2,4},{3,35},{4,6},{5,37},{6,0},{7,39},{8,10},{9,41},... | collective-permute-start | bytes 983048 | tf_op jit(solution)/shard_map/ppermute | solution.py:485
  41.6 28.4 %collective-permute-start.9 = (bf16[5,128,256]{2,1,0:T(8,128)(2,1)}, bf16[5,128,256]{2,1,0:T(8,128)(2,1)}, u32[]{:S(2)}, u32[]{:S(2)}) collective-permute-start(bf16[5,128,256]{2,1,0:T(8,128)(2,1)} %pad_maximum_fusion.refs_3_), channel_id=1, source_target_pairs={{0,1},{1,0},{2,3},{3,2},{4,5},{5,4},{6,7},{7,6},{8,9},{9,8},{10,11... | collective-permute-start | bytes 983048 | tf_op jit(solution)/shard_map/ppermute | solution.py:498
  41.7 28.3 %collective-permute-start.12 = (bf16[5,128,256]{2,1,0:T(8,128)(2,1)}, bf16[5,128,256]{2,1,0:T(8,128)(2,1)}, u32[]{:S(2)}, u32[]{:S(2)}) collective-permute-start(bf16[5,128,256]{2,1,0:T(8,128)(2,1)} %collective-permute-done.8.refs_6_), channel_id=1, source_target_pairs={{0,1},{1,0},{2,3},{3,2},{4,5},{5,4},{6,7},{7,6},{8,9},{9,8},{10,11... | collective-permute-start | bytes 983048 | tf_op jit(solution)/shard_map/ppermute | solution.py:498
  42.2 27.8 %collective-permute-start.11 = (bf16[5,128,256]{2,1,0:T(8,128)(2,1)}, bf16[5,128,256]{2,1,0:T(8,128)(2,1)}, u32[]{:S(2)}, u32[]{:S(2)}) collective-permute-start(bf16[5,128,256]{2,1,0:T(8,128)(2,1)} %collective-permute-done.7.refs_5_), channel_id=1, source_target_pairs={{0,1},{1,0},{2,3},{3,2},{4,5},{5,4},{6,7},{7,6},{8,9},{9,8},{10,11... | collective-permute-start | bytes 983048 | tf_op jit(solution)/shard_map/ppermute | solution.py:498
  42.7 27.4 %collective-permute-start.10 = (bf16[5,128,256]{2,1,0:T(8,128)(2,1)}, bf16[5,128,256]{2,1,0:T(8,128)(2,1)}, u32[]{:S(2)}, u32[]{:S(2)}) collective-permute-start(bf16[5,128,256]{2,1,0:T(8,128)(2,1)} %collective-permute-done.6.refs_4_), channel_id=1, source_target_pairs={{0,1},{1,0},{2,3},{3,2},{4,5},{5,4},{6,7},{7,6},{8,9},{9,8},{10,11... | collective-permute-start | bytes 983048 | tf_op jit(solution)/shard_map/ppermute | solution.py:498

commit v4 on v3

--- a/solution.py
+++ b/solution.py
@@ -190,6 +190,8 @@
             all_hbm.at[pl.ds(block * n, n), :], target.at[:, pl.ds(j * 256, 256)], sems.at[sem]
         )
 
+    for pair in range(HEADS // 2):
+        val_ref[pair, :, 128:] = jnp.ones((slots, 128), BF16)
     get_got.wait()
     get_count = [get_block(12 + j, count_ref, j, 8 + j) for j in range(4)]
     gets = [get_block(8 + j, query_ref, j, 2 + j) for j in range(2)]
@@ -208,67 +210,75 @@
     for pair in range(HEADS // 2):
         lo = d + pair * 128
         val_ref[pair, :, :128] = kv[:, lo : lo + 128]
-        val_ref[pair, :, 128:] = jnp.ones((slots, 128), BF16)
     for copy in get_count:
         copy.wait()
-    count = count_ref[...].astype(F32)
-    bias_ref[...] = jnp.where((count > 0.0) & (empty < 0.5), jnp.log2(jnp.maximum(count, 1.0)), NEG)
     for copy in gets:
         copy.wait()
 
-    def attend(step, exact):
+    def attend(i, step, exact):
         lane = lax.broadcasted_iota(jnp.int32, (step, 128), 1)
-
-        def body(i, carry):
-            at = pl.ds(pl.multiple_of(i * step, step), step)
-            own = own_ref[at, :]
-            tops = own
-            sums = jnp.ones((step, 128), F32)
-            for pair in range(HEADS // 2):
-                lo = pair * 128
-                sides = []
-                for odd in range(2):
-                    head = 2 * pair + odd
-                    scores = lax.dot_general(
-                        one_head(query_ref[at, lo : lo + 128], odd),
-                        key_ref[:, lo : lo + 128],
-                        NT,
-                        preferred_element_type=F32,
-                    )
-                    scores = scores * LOG2E + bias_ref[at, :]
-                    shift = own[:, head : head + 1]
-                    if exact:
-                        mine = shift
-                        shift = jnp.maximum(jnp.max(scores, axis=1, keepdims=True), mine)
-                        self_weight = jnp.exp2(mine - shift).astype(BF16).astype(F32)
-                        tops = jnp.where(lane == head, shift, tops)
-                    else:
-                        self_weight = 1.0
-                    weights = jnp.exp2(scores - shift).astype(BF16)
-                    part = jnp.dot(weights, val_ref[pair], preferred_element_type=F32)
-                    sums = jnp.where(lane == head, part[:, 128:] + self_weight, sums)
-                    sides.append(part[:, :128] + self_weight * value_ref[at, lo : lo + 128].astype(F32))
-                acc_ref[at, lo : lo + 128] = jnp.where(lane < 64, sides[0], sides[1])
-            top_ref[at, :] = tops
-            sum_ref[at, :] = sums
-            return carry
-
-        lax.fori_loop(0, n // step, body, 0)
-
-    attend(256, False)
+        at = pl.ds(pl.multiple_of(i * step, step), step)
+        count = count_ref[at, :].astype(F32)
+        listed = (count > 0.0) & (empty < 0.5)
+        bias_ref[at, :] = jnp.where(listed, jnp.log2(jnp.maximum(count, 1.0)), NEG)
+        own = own_ref[at, :]
+        tops = own
+        sums = jnp.ones((step, 128), F32)
+        for pair in range(HEADS // 2):
+            lo = pair * 128
+            sides = []
+            for odd in range(2):
+                head = 2 * pair + odd
+                scores = lax.dot_general(
+                    one_head(query_ref[at, lo : lo + 128], odd),
+                    key_ref[:, lo : lo + 128],
+                    NT,
+                    preferred_element_type=F32,
+                )
+                scores = scores * LOG2E + bias_ref[at, :]
+                shift = own[:, head : head + 1]
+                if exact:
+                    mine = shift
+                    shift = jnp.maximum(jnp.max(scores, axis=1, keepdims=True), mine)
+                    self_weight = jnp.exp2(mine - shift).astype(BF16).astype(F32)
+                    tops = jnp.where(lane == head, shift, tops)
+                else:
+                    self_weight = 1.0
+                weights = jnp.exp2(scores - shift).astype(BF16)
+                part = jnp.dot(weights, val_ref[pair], preferred_element_type=F32)
+                sums = jnp.where(lane == head, part[:, 128:] + self_weight, sums)
+                sides.append(part[:, :128] + self_weight * value_ref[at, lo : lo + 128].astype(F32))
+            acc_ref[at, lo : lo + 128] = jnp.where(lane < 64, sides[0], sides[1])
+        top_ref[at, :] = tops
+        sum_ref[at, :] = sums
+
+    half = n // 2
+
+    def results(i):
+        at = pl.ds(pl.multiple_of(i * half, half), half)
+        return [
+            pltpu.make_async_copy(source.at[at, :], target.at[at, :], sems.at[12 + 3 * i + j])
+            for j, (source, target) in enumerate(
+                ((top_ref, top_hbm), (sum_ref, sum_hbm), (acc_ref, acc_hbm))
+            )
+        ]
+
+    for i in range(2):
+        attend(i, half, False)
+        for copy in results(i):
+            copy.start()
+    for i in range(2):
+        for copy in results(i):
+            copy.wait()
     worst = jnp.max(jnp.max(sum_ref[...], axis=0, keepdims=True))
 
     @pl.when(jnp.logical_not(worst < BIG))
     def _():
-        attend(64, True)
-
-    puts = [
-        start_copy(top_ref, top_hbm, sems.at[12]),
-        start_copy(sum_ref, sum_hbm, sems.at[13]),
-        start_copy(acc_ref, acc_hbm, sems.at[14]),
-    ]
-    for copy in puts:
-        copy.wait()
+        lax.fori_loop(0, n // 64, lambda i, carry: attend(i, 64, True) or carry, 0)
+        for i in range(2):
+            for copy in results(i):
+                copy.start()
+                copy.wait()
 
 
 def near_attend(got, w, everything, own):
@@ -287,7 +297,7 @@
             pltpu.VMEM((slots, d), BF16),
             pltpu.VMEM((HEADS // 2, slots, 256), BF16),
             pltpu.VMEM((n, slots), F32),
-            pltpu.SemaphoreType.DMA((15,)),
+            pltpu.SemaphoreType.DMA((18,)),
         ],
         compiler_params=params(67043328),
         cost_estimate=pl.CostEstimate(flops=5 * 10**9, bytes_accessed=5 * 10**6, transcendentals=10**6),
@@ -403,26 +413,48 @@
     for copy in late:
         copy.wait()
     lane = lax.broadcasted_iota(jnp.int32, (n, 128), 1)
-    for pair in range(HEADS // 2):
-        lo = pair * 128
-        sides = []
-        for odd in range(2):
-            head = 2 * pair + odd
-            at = pl.ds(head * n, n)
-            shift = shift_ref[at, :1]
-            top = top_ref[:, head : head + 1]
-            best = jnp.maximum(shift, top)
-            disk_scale = jnp.exp2(shift - best)
-            near_scale = jnp.exp2(top - best)
-            total = (
-                jnp.sum(den_ref[at, :], axis=1, keepdims=True) * disk_scale
-                + sum_ref[:, head : head + 1] * near_scale
-            )
-            inv = 1.0 / total
-            mixed = (acc_ref[at, :] * (disk_scale * inv)).astype(BF16)
-            part = jnp.dot(mixed, wd_ref[:, d + lo : d + lo + 128], preferred_element_type=F32)
-            sides.append(part + near_ref[:, lo : lo + 128] * (near_scale * inv))
-        att_ref[:, lo : lo + 128] = jnp.where(lane < 64, sides[0], sides[1]).astype(BF16)
+
+    def join(scaled):
+        for pair in range(HEADS // 2):
+            lo = pair * 128
+            sides = []
+            for odd in range(2):
+                head = 2 * pair + odd
+                at = pl.ds(head * n, n)
+                wide = acc_ref[at, :]
+                part_sum = den_ref[at, :]
+                near = near_ref[:, lo : lo + 128]
+                near_sum = sum_ref[...]
+                if scaled:
+                    shift = shift_ref[at, :1]
+                    top = top_ref[:, head : head + 1]
+                    best = jnp.maximum(shift, top)
+                    disk_scale = jnp.exp2(shift - best)
+                    near_scale = jnp.exp2(top - best)
+                    wide = wide * disk_scale
+                    part_sum = part_sum * disk_scale
+                    near = near * near_scale
+                    near_sum = near_sum * near_scale
+                total = jnp.sum(
+                    part_sum + jnp.where(lane == head, near_sum, 0.0), axis=1, keepdims=True
+                )
+                part = jnp.dot(
+                    wide.astype(BF16), wd_ref[:, d + lo : d + lo + 128], preferred_element_type=F32
+                )
+                sides.append((part + near) * (1.0 / total))
+            att_ref[:, lo : lo + 128] = jnp.where(lane < 64, sides[0], sides[1]).astype(BF16)
+
+    moved = jnp.max(jnp.max(jnp.abs(top_ref[...] - own_ref[...]), axis=0, keepdims=True))
+    same = (worst < BIG) & (moved == 0.0)
+
+    @pl.when(same)
+    def _():
+        join(False)
+
+    @pl.when(jnp.logical_not(same))
+    def _():
+        join(True)
+
     out = jnp.dot(att_ref[...], wout_ref[...], preferred_element_type=F32)
     out_ref[...] = (x_ref[...].astype(F32) + out).astype(BF16)
 

time: 99.7 us -> 102 us (1.023)
  Pallas kernels: 66.1 us -> 68.4 us
    pallas_call x1, Pallas kernels: 25.9 us -> 30 us  [near_attend(): pl.pallas_call(near_kernel, out_shape=tuple((shape(*o) for o in outs)), i...]
    pallas_call x1, Pallas kernels: 29.1 us -> 27.3 us  [disk_attend(): pl.pallas_call(functools.partial(disk_kernel, pieces=len(pieces)), out_sh...]
  transfers between devices with their start and end apart: 14 -> 14, of which waited for: 2 -> 2; matrix products, arithmetic and copies ran while one was open for 2% -> 2% of each run, Pallas kernels for 37% -> 40%
where the time goes in v4:
time: 102 us
  Pallas kernels  68.4 us (67%)
  starting transfers between devices  25.9 us (25%)
  waiting for transfers between devices  3.92 us (4%)
  other arithmetic  3.13 us (3%)
    pallas_call x1, Pallas kernels, near_attend(): pl.pallas_call(near_kernel, out_shape=tuple((shape(*o) for o in outs)), i...  30 us
    pallas_call x1, Pallas kernels, disk_attend(): pl.pallas_call(functools.partial(disk_kernel, pieces=len(pieces)), out_sh...  27.3 us
    ppermute x9, starting transfers between devices, spread(): got.append(lax.ppermute(block, AXES, ring((first, by), (second, by))))  15.7 us
    pallas_call x1, Pallas kernels, prep(): pl.pallas_call(prep_kernel, out_shape=tuple((shape(*o) for o in outs)), i...  8.44 us
    all_to_all x1, starting transfers between devices, local(): lax.all_to_all(send.reshape(devices, 8, width), AXES, split_axis=0, conca...  7.8 us
    ppermute x9, waiting for transfers between devices, spread(): got.append(lax.ppermute(block, AXES, ring((first, by), (second, by))))  3.91 us
    pallas_call x1, Pallas kernels, place(): pl.pallas_call(place_kernel, out_shape=shape((slots, rows.shape[1]), BF16...  2.64 us
    ppermute x4, starting transfers between devices, gather_tokens(): swapped.append(lax.ppermute(piece, AXES, other_core()))  2.42 us
  transfers between devices with their start and end apart: 14, of which 2 were waited for; matrix products, arithmetic and copies ran while one was open for 2% of the time, Pallas kernels for 40%

profile of v4, /device:TPU:0, one launch (start us, length us, event | category | flops | bytes accessed | tf_op | source)
XLA Modules:
  0.0 101.6 jit_solution(2625563370177035582)
XLA Ops:
  0.0 4.0 %collective-permute-start.2 = (bf16[5,8,256]{2,1,0:T(8,128)(2,1)}, bf16[5,8,256]{2,1,0:T(8,128)(2,1)S(1)}, u32[]{:S(2)}, u32[]{:S(2)}) collective-permute-start(bf16[5,8,256]{2,1,0:T(8,128)(2,1)} %bitcast.8), channel_id=1, source_target_pairs={{0,64},{1,17},{2,66},{3,19},{4,68},{5,21},{6,70},{7,23},{8,72},{9,... | collective-permute-start | bytes 61448 | tf_op jit(solution)/shard_map/ppermute | solution.py:517
  4.0 0.7 collective-permute-start.1
  4.7 1.3 %collective-permute-start = (bf16[5,8,256]{2,1,0:T(8,128)(2,1)}, bf16[5,8,256]{2,1,0:T(8,128)(2,1)S(1)}, u32[]{:S(2)}, u32[]{:S(2)}) collective-permute-start(bf16[5,8,256]{2,1,0:T(8,128)(2,1)} %bitcast.10), channel_id=1, source_target_pairs={{0,32},{1,9},{2,34},{3,11},{4,36},{5,13},{6,38},{7,15},{8,40},{9,1... | collective-permute-start | bytes 61448 | tf_op jit(solution)/shard_map/ppermute | solution.py:517
  6.0 0.0 collective-permute-done.2
  6.0 2.0 %collective-permute-done.1 = bf16[5,8,256]{2,1,0:T(8,128)(2,1)S(1)} collective-permute-done((bf16[5,8,256]{2,1,0:T(8,128)(2,1)}, bf16[5,8,256]{2,1,0:T(8,128)(2,1)S(1)}, u32[]{:S(2)}, u32[]{:S(2)}) %collective-permute-start.1) | collective-permute-done | bytes 20512 | tf_op jit(solution)/shard_map/ppermute | solution.py:517
  8.0 1.9 %collective-permute-done = bf16[5,8,256]{2,1,0:T(8,128)(2,1)S(1)} collective-permute-done((bf16[5,8,256]{2,1,0:T(8,128)(2,1)}, bf16[5,8,256]{2,1,0:T(8,128)(2,1)S(1)}, u32[]{:S(2)}, u32[]{:S(2)}) %collective-permute-start) | collective-permute-done | bytes 20512 | tf_op jit(solution)/shard_map/ppermute | solution.py:517
  9.9 1.4 %pad_maximum_fusion.1 = bf16[5,32,256]{2,1,0:T(8,128)(2,1)} fusion(bf16[5,8,256]{2,1,0:T(8,128)(2,1)S(1)} %collective-permute-done.2, bf16[5,8,256]{2,1,0:T(8,128)(2,1)S(1)} %collective-permute-done.1, bf16[5,8,256]{2,1,0:T(8,128)(2,1)S(1)} %collective-permute-done, bf16[5,8,256]{2,1,0:T(8,128)(2,1)} %bitcast.11), kind=kLoop, calls=%fused_computation.1 | loop fusion | flops 327680 | bytes 163840 | tf_op jit(solution)/shard_map/concatenate | solution.py:523
  11.3 3.2 %collective-permute-start.5 = (bf16[5,32,256]{2,1,0:T(8,128)(2,1)}, bf16[5,32,256]{2,1,0:T(8,128)(2,1)}, u32[]{:S(2)}, u32[]{:S(2)}) collective-permute-start(bf16[5,32,256]{2,1,0:T(8,128)(2,1)} %pad_maximum_fusion.1), channel_id=1, source_target_pairs={{0,16},{1,5},{2,18},{3,7},{4,20},{5,1},{6,22},{7,3},{8,24},{9,13},... | collective-permute-start | bytes 245768 | tf_op jit(solution)/shard_map/ppermute | solution.py:517
  14.5 1.1 %collective-permute-start.4 = (bf16[5,32,256]{2,1,0:T(8,128)(2,1)}, bf16[5,32,256]{2,1,0:T(8,128)(2,1)}, u32[]{:S(2)}, u32[]{:S(2)}) collective-permute-start(bf16[5,32,256]{2,1,0:T(8,128)(2,1)} %pad_maximum_fusion.1), channel_id=1, source_target_pairs={{0,24},{1,7},{2,26},{3,1},{4,28},{5,3},{6,30},{7,5},{8,0},{9,15},{... | collective-permute-start | bytes 245768 | tf_op jit(solution)/shard_map/ppermute | solution.py:517
  15.5 1.0 collective-permute-start.3
  16.5 2.6 %place.1 = bf16[1024,256]{1,0:T(8,128)(2,1)} custom-call(s32[1,512]{1,0:T(1,128)} %bitcast.14, bf16[512,256]{1,0:T(8,128)(2,1)} %rows_ref.1), custom_call_target="tpu_custom_call" | custom-call | flops 1000000000 | bytes 1000000 | tf_op jit(solution)/shard_map/place/pallas_call | solution.py:71
  19.1 7.8 %all-to-all-start = ((bf16[128,8,256]{2,1,0:T(8,128)(2,1)}), bf16[128,8,256]{2,1,0:T(8,128)(2,1)}, u32[]{:S(2)}, u32[]{:S(2)}) async-start(bf16[128,8,256]{2,1,0:T(8,128)(2,1)} %bitcast.7), calls=%async_computation | async-start | bytes 1048576 | tf_op jit(solution)/shard_map/all_to_all | solution.py:554
  27.0 0.0 collective-permute-done.5
  27.0 1.8 %pad_maximum_fusion.refs_3_ = bf16[5,128,256]{2,1,0:T(8,128)(2,1)} fusion(bf16[5,32,256]{2,1,0:T(8,128)(2,1)} %collective-permute-done.5, bf16[5,32,256]{2,1,0:T(8,128)(2,1)} %collective-permute-done.4, bf16[5,32,256]{2,1,0:T(8,128)(2,1)} %collective-permute-done.3, bf16[5,32,256]{2,1,0:T(8,128)(2,1)} %pad_maximum_fusion.1), kind=kLoop, calls=%fused_computation | loop fusion | flops 1310720 | bytes 655360 | tf_op jit(solution)/shard_map/concatenate | solution.py:525
  28.7 2.4 %collective-permute-start.8 = (bf16[5,128,256]{2,1,0:T(8,128)(2,1)}, bf16[5,128,256]{2,1,0:T(8,128)(2,1)}, u32[]{:S(2)}, u32[]{:S(2)}) collective-permute-start(bf16[5,128,256]{2,1,0:T(8,128)(2,1)} %pad_maximum_fusion.refs_3_), channel_id=1, source_target_pairs={{0,4},{1,65},{2,6},{3,67},{4,0},{5,69},{6,2},{7,71},{8,12},{9,73},... | collective-permute-start | bytes 983048 | tf_op jit(solution)/shard_map/ppermute | solution.py:517
  31.1 1.2 %collective-permute-start.7 = (bf16[5,128,256]{2,1,0:T(8,128)(2,1)}, bf16[5,128,256]{2,1,0:T(8,128)(2,1)}, u32[]{:S(2)}, u32[]{:S(2)}) collective-permute-start(bf16[5,128,256]{2,1,0:T(8,128)(2,1)} %pad_maximum_fusion.refs_3_), channel_id=1, source_target_pairs={{0,6},{1,97},{2,0},{3,99},{4,2},{5,101},{6,4},{7,103},{8,14},{9,10... | collective-permute-start | bytes 983048 | tf_op jit(solution)/shard_map/ppermute | solution.py:517
  32.3 0.9 collective-permute-start.6
  33.2 8.4 %prep.1 = (bf16[8192,256]{1,0:T(8,128)(2,1)}, f32[512,128]{1,0:T(8,128)}) custom-call(s32[32,512]{1,0:T(8,128)} %bitcast.12, s32[32,512]{1,0:T(8,128)} %bitcast.13, bf16[512,512]{1,0:T(8,128)(2,1)} %refs_17_.1, f32[1,512]{1,0:T(1,128)} %bitcast.15, bf16[512,512]{1,0:T(8,128)(2,1)} %wq_hbm.1, bf16[512,1024]{1,0:T(8,128)(2,1)} %wkv_hbm.1, ...), custom_call_target="tpu_custom_call" | custom-call | flops 8000000000 | bytes 8000000 | tf_op jit(solution)/shard_map/prep/pallas_call | solution.py:161
  41.6 0.1 collective-permute-start.9
  41.7 0.5 collective-permute-start.12
  42.2 0.4 collective-permute-start.11
  42.7 1.4 %collective-permute-start.10 = (bf16[5,128,256]{2,1,0:T(8,128)(2,1)}, bf16[5,128,256]{2,1,0:T(8,128)(2,1)}, u32[]{:S(2)}, u32[]{:S(2)}) collective-permute-start(bf16[5,128,256]{2,1,0:T(8,128)(2,1)} %collective-permute-done.6.refs_4_), channel_id=1, source_target_pairs={{0,1},{1,0},{2,3},{3,2},{4,5},{5,4},{6,7},{7,6},{8,9},{9,8},{10,11... | collective-permute-start | bytes 983048 | tf_op jit(solution)/shard_map/ppermute | solution.py:530
  44.1 30.0 %near_attend.1 = (f32[512,128]{1,0:T(8,128)}, f32[512,128]{1,0:T(8,128)}, f32[512,512]{1,0:T(8,128)}) custom-call(bf16[1024,256]{1,0:T(8,128)(2,1)} %bitcast.6.got_hbm, bf16[256,1024]{1,0:T(8,128)(2,1)} %w_hbm.1, bf16[8192,256]{1,0:T(8,128)(2,1)} %get-tuple-element.10.all_hbm.refs_2_, f32[512,128]{1,0:T(8,128)} %get-tuple-element.11.own_hbm.refs_11_), custom_call_target="tpu_custom_call" | custom-call | flops 5000000000 | bytes 5000000 | tf_op jit(solution)/shard_map/near_attend/pallas_call | solution.py:290
  74.1 27.3 %disk_attend.1 = bf16[512,512]{1,0:T(8,128)(2,1)} custom-call(s32[5]{0:T(128)} %refs_0_.1, s32[5]{0:T(128)} %refs_1_.1, bf16[8192,256]{1,0:T(8,128)(2,1)} %get-tuple-element.10.all_hbm.refs_2_, bf16[5,128,256]{2,1,0:T(8,128)(2,1)} %pad_maximum_fusion.refs_3_, bf16[5,128,256]{2,1,0:T(8,128)(2,1)} %collective-permute-done.6.refs_4_, ...), custom_call_target="tpu_custom_call" | custom-call | flops 16000000000 | bytes 10000000 | tf_op jit(solution)/shard_map/disk_attend/pallas_call | solution.py:468
  (10 shorter events, 0.0 us)
Async XLA Ops:
  0.0 6.0 %collective-permute-start.2 = (bf16[5,8,256]{2,1,0:T(8,128)(2,1)}, bf16[5,8,256]{2,1,0:T(8,128)(2,1)S(1)}, u32[]{:S(2)}, u32[]{:S(2)}) collective-permute-start(bf16[5,8,256]{2,1,0:T(8,128)(2,1)} %bitcast.8), channel_id=1, source_target_pairs={{0,64},{1,17},{2,66},{3,19},{4,68},{5,21},{6,70},{7,23},{8,72},{9,... | collective-permute-start | bytes 61448 | tf_op jit(solution)/shard_map/ppermute | solution.py:517
  4.0 4.0 %collective-permute-start.1 = (bf16[5,8,256]{2,1,0:T(8,128)(2,1)}, bf16[5,8,256]{2,1,0:T(8,128)(2,1)S(1)}, u32[]{:S(2)}, u32[]{:S(2)}) collective-permute-start(bf16[5,8,256]{2,1,0:T(8,128)(2,1)} %bitcast.9), channel_id=1, source_target_pairs={{0,96},{1,25},{2,98},{3,27},{4,100},{5,29},{6,102},{7,31},{8,104},... | collective-permute-start | bytes 61448 | tf_op jit(solution)/shard_map/ppermute | solution.py:517
  4.7 5.2 %collective-permute-start = (bf16[5,8,256]{2,1,0:T(8,128)(2,1)}, bf16[5,8,256]{2,1,0:T(8,128)(2,1)S(1)}, u32[]{:S(2)}, u32[]{:S(2)}) collective-permute-start(bf16[5,8,256]{2,1,0:T(8,128)(2,1)} %bitcast.10), channel_id=1, source_target_pairs={{0,32},{1,9},{2,34},{3,11},{4,36},{5,13},{6,38},{7,15},{8,40},{9,1... | collective-permute-start | bytes 61448 | tf_op jit(solution)/shard_map/ppermute | solution.py:517
  11.3 15.7 %collective-permute-start.5 = (bf16[5,32,256]{2,1,0:T(8,128)(2,1)}, bf16[5,32,256]{2,1,0:T(8,128)(2,1)}, u32[]{:S(2)}, u32[]{:S(2)}) collective-permute-start(bf16[5,32,256]{2,1,0:T(8,128)(2,1)} %pad_maximum_fusion.1), channel_id=1, source_target_pairs={{0,16},{1,5},{2,18},{3,7},{4,20},{5,1},{6,22},{7,3},{8,24},{9,13},... | collective-permute-start | bytes 245768 | tf_op jit(solution)/shard_map/ppermute | solution.py:517
  14.5 12.5 %collective-permute-start.4 = (bf16[5,32,256]{2,1,0:T(8,128)(2,1)}, bf16[5,32,256]{2,1,0:T(8,128)(2,1)}, u32[]{:S(2)}, u32[]{:S(2)}) collective-permute-start(bf16[5,32,256]{2,1,0:T(8,128)(2,1)} %pad_maximum_fusion.1), channel_id=1, source_target_pairs={{0,24},{1,7},{2,26},{3,1},{4,28},{5,3},{6,30},{7,5},{8,0},{9,15},{... | collective-permute-start | bytes 245768 | tf_op jit(solution)/shard_map/ppermute | solution.py:517
  15.5 11.4 %collective-permute-start.3 = (bf16[5,32,256]{2,1,0:T(8,128)(2,1)}, bf16[5,32,256]{2,1,0:T(8,128)(2,1)}, u32[]{:S(2)}, u32[]{:S(2)}) collective-permute-start(bf16[5,32,256]{2,1,0:T(8,128)(2,1)} %pad_maximum_fusion.1), channel_id=1, source_target_pairs={{0,8},{1,3},{2,10},{3,5},{4,12},{5,7},{6,14},{7,1},{8,16},{9,11},{... | collective-permute-start | bytes 245768 | tf_op jit(solution)/shard_map/ppermute | solution.py:517
  19.1 24.9 %all-to-all-start = ((bf16[128,8,256]{2,1,0:T(8,128)(2,1)}), bf16[128,8,256]{2,1,0:T(8,128)(2,1)}, u32[]{:S(2)}, u32[]{:S(2)}) async-start(bf16[128,8,256]{2,1,0:T(8,128)(2,1)} %bitcast.7), calls=%async_computation | async-start | bytes 1048576 | tf_op jit(solution)/shard_map/all_to_all | solution.py:554
  28.7 13.0 %collective-permute-start.8 = (bf16[5,128,256]{2,1,0:T(8,128)(2,1)}, bf16[5,128,256]{2,1,0:T(8,128)(2,1)}, u32[]{:S(2)}, u32[]{:S(2)}) collective-permute-start(bf16[5,128,256]{2,1,0:T(8,128)(2,1)} %pad_maximum_fusion.refs_3_), channel_id=1, source_target_pairs={{0,4},{1,65},{2,6},{3,67},{4,0},{5,69},{6,2},{7,71},{8,12},{9,73},... | collective-permute-start | bytes 983048 | tf_op jit(solution)/shard_map/ppermute | solution.py:517
  31.1 11.1 %collective-permute-start.7 = (bf16[5,128,256]{2,1,0:T(8,128)(2,1)}, bf16[5,128,256]{2,1,0:T(8,128)(2,1)}, u32[]{:S(2)}, u32[]{:S(2)}) collective-permute-start(bf16[5,128,256]{2,1,0:T(8,128)(2,1)} %pad_maximum_fusion.refs_3_), channel_id=1, source_target_pairs={{0,6},{1,97},{2,0},{3,99},{4,2},{5,101},{6,4},{7,103},{8,14},{9,10... | collective-permute-start | bytes 983048 | tf_op jit(solution)/shard_map/ppermute | solution.py:517
  32.3 10.4 %collective-permute-start.6 = (bf16[5,128,256]{2,1,0:T(8,128)(2,1)}, bf16[5,128,256]{2,1,0:T(8,128)(2,1)}, u32[]{:S(2)}, u32[]{:S(2)}) collective-permute-start(bf16[5,128,256]{2,1,0:T(8,128)(2,1)} %pad_maximum_fusion.refs_3_), channel_id=1, source_target_pairs={{0,2},{1,33},{2,4},{3,35},{4,6},{5,37},{6,0},{7,39},{8,10},{9,41},... | collective-permute-start | bytes 983048 | tf_op jit(solution)/shard_map/ppermute | solution.py:517
  41.6 32.4 %collective-permute-start.9 = (bf16[5,128,256]{2,1,0:T(8,128)(2,1)}, bf16[5,128,256]{2,1,0:T(8,128)(2,1)}, u32[]{:S(2)}, u32[]{:S(2)}) collective-permute-start(bf16[5,128,256]{2,1,0:T(8,128)(2,1)} %pad_maximum_fusion.refs_3_), channel_id=1, source_target_pairs={{0,1},{1,0},{2,3},{3,2},{4,5},{5,4},{6,7},{7,6},{8,9},{9,8},{10,11... | collective-permute-start | bytes 983048 | tf_op jit(solution)/shard_map/ppermute | solution.py:530
  41.7 32.3 %collective-permute-start.12 = (bf16[5,128,256]{2,1,0:T(8,128)(2,1)}, bf16[5,128,256]{2,1,0:T(8,128)(2,1)}, u32[]{:S(2)}, u32[]{:S(2)}) collective-permute-start(bf16[5,128,256]{2,1,0:T(8,128)(2,1)} %collective-permute-done.8.refs_6_), channel_id=1, source_target_pairs={{0,1},{1,0},{2,3},{3,2},{4,5},{5,4},{6,7},{7,6},{8,9},{9,8},{10,11... | collective-permute-start | bytes 983048 | tf_op jit(solution)/shard_map/ppermute | solution.py:530
  42.2 31.9 %collective-permute-start.11 = (bf16[5,128,256]{2,1,0:T(8,128)(2,1)}, bf16[5,128,256]{2,1,0:T(8,128)(2,1)}, u32[]{:S(2)}, u32[]{:S(2)}) collective-permute-start(bf16[5,128,256]{2,1,0:T(8,128)(2,1)} %collective-permute-done.7.refs_5_), channel_id=1, source_target_pairs={{0,1},{1,0},{2,3},{3,2},{4,5},{5,4},{6,7},{7,6},{8,9},{9,8},{10,11... | collective-permute-start | bytes 983048 | tf_op jit(solution)/shard_map/ppermute | solution.py:530
  42.7 31.4 %collective-permute-start.10 = (bf16[5,128,256]{2,1,0:T(8,128)(2,1)}, bf16[5,128,256]{2,1,0:T(8,128)(2,1)}, u32[]{:S(2)}, u32[]{:S(2)}) collective-permute-start(bf16[5,128,256]{2,1,0:T(8,128)(2,1)} %collective-permute-done.6.refs_4_), channel_id=1, source_target_pairs={{0,1},{1,0},{2,3},{3,2},{4,5},{5,4},{6,7},{7,6},{8,9},{9,8},{10,11... | collective-permute-start | bytes 983048 | tf_op jit(solution)/shard_map/ppermute | solution.py:530

commit v5 on v4

--- a/solution.py
+++ b/solution.py
@@ -74,7 +74,7 @@
         in_specs=[VMEM, VMEM],
         out_specs=HBM,
         scratch_shapes=[pltpu.VMEM((slots, rows.shape[1]), BF16), pltpu.SemaphoreType.DMA((4,))],
-        compiler_params=params(67043328),
+        compiler_params=params(),
         cost_estimate=pl.CostEstimate(flops=10**9, bytes_accessed=10**6, transcendentals=0),
         name="place",
     )(owner, rows)
@@ -212,15 +212,14 @@
         val_ref[pair, :, :128] = kv[:, lo : lo + 128]
     for copy in get_count:
         copy.wait()
+    count = count_ref[...].astype(F32)
+    bias_ref[...] = jnp.where((count > 0.0) & (empty < 0.5), jnp.log2(jnp.maximum(count, 1.0)), NEG)
     for copy in gets:
         copy.wait()
 
     def attend(i, step, exact):
         lane = lax.broadcasted_iota(jnp.int32, (step, 128), 1)
         at = pl.ds(pl.multiple_of(i * step, step), step)
-        count = count_ref[at, :].astype(F32)
-        listed = (count > 0.0) & (empty < 0.5)
-        bias_ref[at, :] = jnp.where(listed, jnp.log2(jnp.maximum(count, 1.0)), NEG)
         own = own_ref[at, :]
         tops = own
         sums = jnp.ones((step, 128), F32)
@@ -263,10 +262,13 @@
             )
         ]
 
-    for i in range(2):
+    def one_half(i, carry):
         attend(i, half, False)
         for copy in results(i):
             copy.start()
+        return carry
+
+    lax.fori_loop(0, 2, one_half, 0)
     for i in range(2):
         for copy in results(i):
             copy.wait()
@@ -520,11 +522,11 @@
 
 def gather_tokens(disk_tokens):
     block = jnp.transpose(disk_tokens, (1, 0, 2))
+    block = jnp.concatenate([block] + spread(block, 2, 0), axis=1)
+    block = lax.optimization_barrier(block)
     block = jnp.concatenate([block] + spread(block, 0, 1), axis=1)
     block = lax.optimization_barrier(block)
-    block = jnp.concatenate([block] + spread(block, 1, 2), axis=1)
-    block = lax.optimization_barrier(block)
-    pieces = [block] + spread(block, 2, 0)
+    pieces = [block] + spread(block, 1, 2)
     swapped = []
     for piece in pieces:
         swapped.append(lax.ppermute(piece, AXES, other_core()))

time: 102 us -> 99.3 us (0.974)
  starting transfers between devices: 25.9 us -> 23.1 us
  waiting for transfers between devices: 3.92 us -> 5.89 us
  other arithmetic: 3.13 us -> 1.48 us
    ppermute x9, waiting for transfers between devices: 3.91 us -> 5.87 us  [spread(): got.append(lax.ppermute(block, AXES, ring((first, by), (second, by))))]
    ppermute x4, starting transfers between devices: 2.42 us -> 0.58 us  [gather_tokens(): swapped.append(lax.ppermute(piece, AXES, other_core()))]
    concatenate x1, other arithmetic: 1.76 us -> 0.73 us  [gather_tokens(): block = jnp.concatenate([block] + spread(block, 2, 0), axis=1)]
  transfers between devices with their start and end apart: 14 -> 14, of which waited for: 2 -> 5; matrix products, arithmetic and copies ran while one was open for 2% -> 1% of each run, Pallas kernels for 40% -> 41%
where the time goes in v5:
time: 99.3 us; the launch traced here: 99 us
  Pallas kernels  68.2 us (69%)
  starting transfers between devices  23.1 us (23%)
  waiting for transfers between devices  5.89 us (6%)
  other arithmetic  1.48 us (1%)
    pallas_call x1, Pallas kernels, near_attend(): pl.pallas_call(near_kernel, out_shape=tuple((shape(*o) for o in outs)), i...  29.6 us
    pallas_call x1, Pallas kernels, disk_attend(): pl.pallas_call(functools.partial(disk_kernel, pieces=len(pieces)), out_sh...  27.6 us
    ppermute x9, starting transfers between devices, spread(): got.append(lax.ppermute(block, AXES, ring((first, by), (second, by))))  15.5 us
    pallas_call x1, Pallas kernels, prep(): pl.pallas_call(prep_kernel, out_shape=tuple((shape(*o) for o in outs)), i...  8.45 us
    all_to_all x1, starting transfers between devices, local(): lax.all_to_all(send.reshape(devices, 8, width), AXES, split_axis=0, conca...  7.03 us
    ppermute x9, waiting for transfers between devices, spread(): got.append(lax.ppermute(block, AXES, ring((first, by), (second, by))))  5.87 us
    pallas_call x1, Pallas kernels, place(): pl.pallas_call(place_kernel, out_shape=shape((slots, rows.shape[1]), BF16...  2.64 us
  transfers between devices with their start and end apart: 14, of which 5 were waited for; matrix products, arithmetic and copies ran while one was open for 1% of the time, Pallas kernels for 41%

profile of v5, /device:TPU:0, one launch (start us, length us, event | category | flops | bytes accessed | tf_op | source)
XLA Modules:
  0.0 99.0 jit_solution(6850024401863651377)
XLA Ops:
  0.0 3.1 %collective-permute-start.2 = (bf16[5,8,256]{2,1,0:T(8,128)(2,1)}, bf16[5,8,256]{2,1,0:T(8,128)(2,1)S(1)}, u32[]{:S(2)}, u32[]{:S(2)}) collective-permute-start(bf16[5,8,256]{2,1,0:T(8,128)(2,1)} %bitcast.8), channel_id=1, source_target_pairs={{0,4},{1,65},{2,6},{3,67},{4,0},{5,69},{6,2},{7,71},{8,12},{9,73},... | collective-permute-start | bytes 61448 | tf_op jit(solution)/shard_map/ppermute | solution.py:519
  3.1 1.1 %collective-permute-start.1 = (bf16[5,8,256]{2,1,0:T(8,128)(2,1)}, bf16[5,8,256]{2,1,0:T(8,128)(2,1)S(1)}, u32[]{:S(2)}, u32[]{:S(2)}) collective-permute-start(bf16[5,8,256]{2,1,0:T(8,128)(2,1)} %bitcast.9), channel_id=1, source_target_pairs={{0,6},{1,97},{2,0},{3,99},{4,2},{5,101},{6,4},{7,103},{8,14},{9,10... | collective-permute-start | bytes 61448 | tf_op jit(solution)/shard_map/ppermute | solution.py:519
  4.3 0.9 collective-permute-start
  5.2 0.3 collective-permute-done.2
  5.5 1.6 %collective-permute-done.1 = bf16[5,8,256]{2,1,0:T(8,128)(2,1)S(1)} collective-permute-done((bf16[5,8,256]{2,1,0:T(8,128)(2,1)}, bf16[5,8,256]{2,1,0:T(8,128)(2,1)S(1)}, u32[]{:S(2)}, u32[]{:S(2)}) %collective-permute-start.1) | collective-permute-done | bytes 20512 | tf_op jit(solution)/shard_map/ppermute | solution.py:519
  7.1 2.4 %collective-permute-done = bf16[5,8,256]{2,1,0:T(8,128)(2,1)S(1)} collective-permute-done((bf16[5,8,256]{2,1,0:T(8,128)(2,1)}, bf16[5,8,256]{2,1,0:T(8,128)(2,1)S(1)}, u32[]{:S(2)}, u32[]{:S(2)}) %collective-permute-start) | collective-permute-done | bytes 20512 | tf_op jit(solution)/shard_map/ppermute | solution.py:519
  9.5 0.7 pad_maximum_fusion.1
  10.2 3.9 %collective-permute-start.5 = (bf16[5,32,256]{2,1,0:T(8,128)(2,1)S(1)}, bf16[5,32,256]{2,1,0:T(8,128)(2,1)S(1)}, u32[]{:S(2)}, u32[]{:S(2)}) collective-permute-start(bf16[5,32,256]{2,1,0:T(8,128)(2,1)S(1)} %pad_maximum_fusion.1), channel_id=1, source_target_pairs={{0,64},{1,17},{2,66},{3,19},{4,68},{5,21},{6,70},{7,23},{8,72},{9,... | collective-permute-start | bytes 245768 | tf_op jit(solution)/shard_map/ppermute | solution.py:519
  14.1 0.7 collective-permute-start.4
  14.8 1.3 %collective-permute-start.3 = (bf16[5,32,256]{2,1,0:T(8,128)(2,1)S(1)}, bf16[5,32,256]{2,1,0:T(8,128)(2,1)S(1)}, u32[]{:S(2)}, u32[]{:S(2)}) collective-permute-start(bf16[5,32,256]{2,1,0:T(8,128)(2,1)S(1)} %pad_maximum_fusion.1), channel_id=1, source_target_pairs={{0,32},{1,9},{2,34},{3,11},{4,36},{5,13},{6,38},{7,15},{8,40},{9,1... | collective-permute-start | bytes 245768 | tf_op jit(solution)/shard_map/ppermute | solution.py:519
  16.1 2.6 %place.1 = bf16[1024,256]{1,0:T(8,128)(2,1)} custom-call(s32[1,512]{1,0:T(1,128)} %bitcast.14, bf16[512,256]{1,0:T(8,128)(2,1)} %rows_ref.1), custom_call_target="tpu_custom_call" | custom-call | flops 1000000000 | bytes 1000000 | tf_op jit(solution)/shard_map/place/pallas_call | solution.py:71
  18.8 7.0 %all-to-all-start = ((bf16[128,8,256]{2,1,0:T(8,128)(2,1)}), bf16[128,8,256]{2,1,0:T(8,128)(2,1)}, u32[]{:S(2)}, u32[]{:S(2)}) async-start(bf16[128,8,256]{2,1,0:T(8,128)(2,1)} %bitcast.7), calls=%async_computation | async-start | bytes 1048576 | tf_op jit(solution)/shard_map/all_to_all | solution.py:556
  25.8 0.7 pad_maximum_fusion.refs_3_
  26.6 2.4 %collective-permute-start.8 = (bf16[5,128,256]{2,1,0:T(8,128)(2,1)}, bf16[5,128,256]{2,1,0:T(8,128)(2,1)}, u32[]{:S(2)}, u32[]{:S(2)}) collective-permute-start(bf16[5,128,256]{2,1,0:T(8,128)(2,1)} %pad_maximum_fusion.refs_3_), channel_id=1, source_target_pairs={{0,16},{1,5},{2,18},{3,7},{4,20},{5,1},{6,22},{7,3},{8,24},{9,13},... | collective-permute-start | bytes 983048 | tf_op jit(solution)/shard_map/ppermute | solution.py:519
  29.0 1.2 %collective-permute-start.7 = (bf16[5,128,256]{2,1,0:T(8,128)(2,1)}, bf16[5,128,256]{2,1,0:T(8,128)(2,1)}, u32[]{:S(2)}, u32[]{:S(2)}) collective-permute-start(bf16[5,128,256]{2,1,0:T(8,128)(2,1)} %pad_maximum_fusion.refs_3_), channel_id=1, source_target_pairs={{0,24},{1,7},{2,26},{3,1},{4,28},{5,3},{6,30},{7,5},{8,0},{9,15},{... | collective-permute-start | bytes 983048 | tf_op jit(solution)/shard_map/ppermute | solution.py:519
  30.1 0.9 collective-permute-start.6
  31.0 8.4 %prep.1 = (bf16[8192,256]{1,0:T(8,128)(2,1)}, f32[512,128]{1,0:T(8,128)}) custom-call(s32[32,512]{1,0:T(8,128)} %bitcast.12, s32[32,512]{1,0:T(8,128)} %bitcast.13, bf16[512,512]{1,0:T(8,128)(2,1)} %refs_17_.1, f32[1,512]{1,0:T(1,128)} %bitcast.15, bf16[512,512]{1,0:T(8,128)(2,1)} %wq_hbm.1, bf16[512,1024]{1,0:T(8,128)(2,1)} %wkv_hbm.1, ...), custom_call_target="tpu_custom_call" | custom-call | flops 8000000000 | bytes 8000000 | tf_op jit(solution)/shard_map/prep/pallas_call | solution.py:161
  39.5 0.1 collective-permute-start.9
  39.6 0.5 collective-permute-start.12
  40.1 0.2 collective-permute-done.7.refs_5_
  40.2 1.4 %collective-permute-done.6.refs_4_ = bf16[5,128,256]{2,1,0:T(8,128)(2,1)} collective-permute-done((bf16[5,128,256]{2,1,0:T(8,128)(2,1)}, bf16[5,128,256]{2,1,0:T(8,128)(2,1)}, u32[]{:S(2)}, u32[]{:S(2)}) %collective-permute-start.6) | collective-permute-done | bytes 327712 | tf_op jit(solution)/shard_map/ppermute | solution.py:519
  41.6 0.0 collective-permute-start.10
  41.6 29.6 %near_attend.1 = (f32[512,128]{1,0:T(8,128)}, f32[512,128]{1,0:T(8,128)}, f32[512,512]{1,0:T(8,128)}) custom-call(bf16[1024,256]{1,0:T(8,128)(2,1)} %bitcast.6.got_hbm, bf16[256,1024]{1,0:T(8,128)(2,1)} %w_hbm.1, bf16[8192,256]{1,0:T(8,128)(2,1)} %get-tuple-element.10.all_hbm.refs_2_, f32[512,128]{1,0:T(8,128)} %get-tuple-element.11.own_hbm.refs_11_), custom_call_target="tpu_custom_call" | custom-call | flops 5000000000 | bytes 5000000 | tf_op jit(solution)/shard_map/near_attend/pallas_call | solution.py:292
  71.3 27.6 %disk_attend.1 = bf16[512,512]{1,0:T(8,128)(2,1)} custom-call(s32[5]{0:T(128)} %refs_0_.1, s32[5]{0:T(128)} %refs_1_.1, bf16[8192,256]{1,0:T(8,128)(2,1)} %get-tuple-element.10.all_hbm.refs_2_, bf16[5,128,256]{2,1,0:T(8,128)(2,1)} %pad_maximum_fusion.refs_3_, bf16[5,128,256]{2,1,0:T(8,128)(2,1)} %collective-permute-done.6.refs_4_, ...), custom_call_target="tpu_custom_call" | custom-call | flops 16000000000 | bytes 10000000 | tf_op jit(solution)/shard_map/disk_attend/pallas_call | solution.py:470
  (10 shorter events, 0.0 us)
Async XLA Ops:
  0.0 5.5 %collective-permute-start.2 = (bf16[5,8,256]{2,1,0:T(8,128)(2,1)}, bf16[5,8,256]{2,1,0:T(8,128)(2,1)S(1)}, u32[]{:S(2)}, u32[]{:S(2)}) collective-permute-start(bf16[5,8,256]{2,1,0:T(8,128)(2,1)} %bitcast.8), channel_id=1, source_target_pairs={{0,4},{1,65},{2,6},{3,67},{4,0},{5,69},{6,2},{7,71},{8,12},{9,73},... | collective-permute-start | bytes 61448 | tf_op jit(solution)/shard_map/ppermute | solution.py:519
  3.1 4.0 %collective-permute-start.1 = (bf16[5,8,256]{2,1,0:T(8,128)(2,1)}, bf16[5,8,256]{2,1,0:T(8,128)(2,1)S(1)}, u32[]{:S(2)}, u32[]{:S(2)}) collective-permute-start(bf16[5,8,256]{2,1,0:T(8,128)(2,1)} %bitcast.9), channel_id=1, source_target_pairs={{0,6},{1,97},{2,0},{3,99},{4,2},{5,101},{6,4},{7,103},{8,14},{9,10... | collective-permute-start | bytes 61448 | tf_op jit(solution)/shard_map/ppermute | solution.py:519
  4.3 5.2 %collective-permute-start = (bf16[5,8,256]{2,1,0:T(8,128)(2,1)}, bf16[5,8,256]{2,1,0:T(8,128)(2,1)S(1)}, u32[]{:S(2)}, u32[]{:S(2)}) collective-permute-start(bf16[5,8,256]{2,1,0:T(8,128)(2,1)} %bitcast.10), channel_id=1, source_target_pairs={{0,2},{1,33},{2,4},{3,35},{4,6},{5,37},{6,0},{7,39},{8,10},{9,41},... | collective-permute-start | bytes 61448 | tf_op jit(solution)/shard_map/ppermute | solution.py:519
  10.2 15.6 %collective-permute-start.5 = (bf16[5,32,256]{2,1,0:T(8,128)(2,1)S(1)}, bf16[5,32,256]{2,1,0:T(8,128)(2,1)S(1)}, u32[]{:S(2)}, u32[]{:S(2)}) collective-permute-start(bf16[5,32,256]{2,1,0:T(8,128)(2,1)S(1)} %pad_maximum_fusion.1), channel_id=1, source_target_pairs={{0,64},{1,17},{2,66},{3,19},{4,68},{5,21},{6,70},{7,23},{8,72},{9,... | collective-permute-start | bytes 245768 | tf_op jit(solution)/shard_map/ppermute | solution.py:519
  14.1 11.7 %collective-permute-start.4 = (bf16[5,32,256]{2,1,0:T(8,128)(2,1)S(1)}, bf16[5,32,256]{2,1,0:T(8,128)(2,1)S(1)}, u32[]{:S(2)}, u32[]{:S(2)}) collective-permute-start(bf16[5,32,256]{2,1,0:T(8,128)(2,1)S(1)} %pad_maximum_fusion.1), channel_id=1, source_target_pairs={{0,96},{1,25},{2,98},{3,27},{4,100},{5,29},{6,102},{7,31},{8,104},... | collective-permute-start | bytes 245768 | tf_op jit(solution)/shard_map/ppermute | solution.py:519
  14.8 11.0 %collective-permute-start.3 = (bf16[5,32,256]{2,1,0:T(8,128)(2,1)S(1)}, bf16[5,32,256]{2,1,0:T(8,128)(2,1)S(1)}, u32[]{:S(2)}, u32[]{:S(2)}) collective-permute-start(bf16[5,32,256]{2,1,0:T(8,128)(2,1)S(1)} %pad_maximum_fusion.1), channel_id=1, source_target_pairs={{0,32},{1,9},{2,34},{3,11},{4,36},{5,13},{6,38},{7,15},{8,40},{9,1... | collective-permute-start | bytes 245768 | tf_op jit(solution)/shard_map/ppermute | solution.py:519
  18.8 22.8 %all-to-all-start = ((bf16[128,8,256]{2,1,0:T(8,128)(2,1)}), bf16[128,8,256]{2,1,0:T(8,128)(2,1)}, u32[]{:S(2)}, u32[]{:S(2)}) async-start(bf16[128,8,256]{2,1,0:T(8,128)(2,1)} %bitcast.7), calls=%async_computation | async-start | bytes 1048576 | tf_op jit(solution)/shard_map/all_to_all | solution.py:556
  26.6 13.0 %collective-permute-start.8 = (bf16[5,128,256]{2,1,0:T(8,128)(2,1)}, bf16[5,128,256]{2,1,0:T(8,128)(2,1)}, u32[]{:S(2)}, u32[]{:S(2)}) collective-permute-start(bf16[5,128,256]{2,1,0:T(8,128)(2,1)} %pad_maximum_fusion.refs_3_), channel_id=1, source_target_pairs={{0,16},{1,5},{2,18},{3,7},{4,20},{5,1},{6,22},{7,3},{8,24},{9,13},... | collective-permute-start | bytes 983048 | tf_op jit(solution)/shard_map/ppermute | solution.py:519
  29.0 11.3 %collective-permute-start.7 = (bf16[5,128,256]{2,1,0:T(8,128)(2,1)}, bf16[5,128,256]{2,1,0:T(8,128)(2,1)}, u32[]{:S(2)}, u32[]{:S(2)}) collective-permute-start(bf16[5,128,256]{2,1,0:T(8,128)(2,1)} %pad_maximum_fusion.refs_3_), channel_id=1, source_target_pairs={{0,24},{1,7},{2,26},{3,1},{4,28},{5,3},{6,30},{7,5},{8,0},{9,15},{... | collective-permute-start | bytes 983048 | tf_op jit(solution)/shard_map/ppermute | solution.py:519
  30.1 11.5 %collective-permute-start.6 = (bf16[5,128,256]{2,1,0:T(8,128)(2,1)}, bf16[5,128,256]{2,1,0:T(8,128)(2,1)}, u32[]{:S(2)}, u32[]{:S(2)}) collective-permute-start(bf16[5,128,256]{2,1,0:T(8,128)(2,1)} %pad_maximum_fusion.refs_3_), channel_id=1, source_target_pairs={{0,8},{1,3},{2,10},{3,5},{4,12},{5,7},{6,14},{7,1},{8,16},{9,11},{... | collective-permute-start | bytes 983048 | tf_op jit(solution)/shard_map/ppermute | solution.py:519
  39.5 31.8 %collective-permute-start.9 = (bf16[5,128,256]{2,1,0:T(8,128)(2,1)}, bf16[5,128,256]{2,1,0:T(8,128)(2,1)}, u32[]{:S(2)}, u32[]{:S(2)}) collective-permute-start(bf16[5,128,256]{2,1,0:T(8,128)(2,1)} %pad_maximum_fusion.refs_3_), channel_id=1, source_target_pairs={{0,1},{1,0},{2,3},{3,2},{4,5},{5,4},{6,7},{7,6},{8,9},{9,8},{10,11... | collective-permute-start | bytes 983048 | tf_op jit(solution)/shard_map/ppermute | solution.py:532
  39.6 31.7 %collective-permute-start.12 = (bf16[5,128,256]{2,1,0:T(8,128)(2,1)}, bf16[5,128,256]{2,1,0:T(8,128)(2,1)}, u32[]{:S(2)}, u32[]{:S(2)}) collective-permute-start(bf16[5,128,256]{2,1,0:T(8,128)(2,1)} %collective-permute-done.8.refs_6_), channel_id=1, source_target_pairs={{0,1},{1,0},{2,3},{3,2},{4,5},{5,4},{6,7},{7,6},{8,9},{9,8},{10,11... | collective-permute-start | bytes 983048 | tf_op jit(solution)/shard_map/ppermute | solution.py:532
  40.2 31.0 %collective-permute-start.11 = (bf16[5,128,256]{2,1,0:T(8,128)(2,1)}, bf16[5,128,256]{2,1,0:T(8,128)(2,1)}, u32[]{:S(2)}, u32[]{:S(2)}) collective-permute-start(bf16[5,128,256]{2,1,0:T(8,128)(2,1)} %collective-permute-done.7.refs_5_), channel_id=1, source_target_pairs={{0,1},{1,0},{2,3},{3,2},{4,5},{5,4},{6,7},{7,6},{8,9},{9,8},{10,11... | collective-permute-start | bytes 983048 | tf_op jit(solution)/shard_map/ppermute | solution.py:532
  41.6 29.6 %collective-permute-start.10 = (bf16[5,128,256]{2,1,0:T(8,128)(2,1)}, bf16[5,128,256]{2,1,0:T(8,128)(2,1)}, u32[]{:S(2)}, u32[]{:S(2)}) collective-permute-start(bf16[5,128,256]{2,1,0:T(8,128)(2,1)} %collective-permute-done.6.refs_4_), channel_id=1, source_target_pairs={{0,1},{1,0},{2,3},{3,2},{4,5},{5,4},{6,7},{7,6},{8,9},{9,8},{10,11... | collective-permute-start | bytes 983048 | tf_op jit(solution)/shard_map/ppermute | solution.py:532

commit v6 on v5

--- a/solution.py
+++ b/solution.py
@@ -513,20 +513,20 @@
     return [(s, s ^ 1) for s in range(128)]
 
 
-def spread(block, first, second):
+def spread(block, first, second, order=(1, 3, 2)):
     got = []
-    for by in (1, 3, 2):
+    for by in order:
         got.append(lax.ppermute(block, AXES, ring((first, by), (second, by))))
     return got
 
 
 def gather_tokens(disk_tokens):
     block = jnp.transpose(disk_tokens, (1, 0, 2))
-    block = jnp.concatenate([block] + spread(block, 2, 0), axis=1)
-    block = lax.optimization_barrier(block)
     block = jnp.concatenate([block] + spread(block, 0, 1), axis=1)
     block = lax.optimization_barrier(block)
-    pieces = [block] + spread(block, 1, 2)
+    block = jnp.concatenate([block] + spread(block, 1, 2), axis=1)
+    block = lax.optimization_barrier(block)
+    pieces = [block] + spread(block, 2, 0, (2, 3, 1))
     swapped = []
     for piece in pieces:
         swapped.append(lax.ppermute(piece, AXES, other_core()))

time: 99.3 us -> 101 us (1.017)
  starting transfers between devices: 23.1 us -> 26.2 us
  waiting for transfers between devices: 5.89 us -> 4.55 us
    ppermute x4, starting transfers between devices: 0.58 us -> 2.81 us  [gather_tokens(): swapped.append(lax.ppermute(piece, AXES, other_core()))]
    ppermute x9, waiting for transfers between devices: 5.87 us -> 4.53 us  [spread(): got.append(lax.ppermute(block, AXES, ring((first, by), (second, by))))]
  transfers between devices with their start and end apart: 14 -> 14, of which waited for: 5 -> 3; matrix products, arithmetic and copies ran while one was open for 1% -> 1% of each run, Pallas kernels for 41% -> 40%
where the time goes in v6:
time: 101 us
  Pallas kernels  68.2 us (68%)
  starting transfers between devices  26.2 us (26%)
  waiting for transfers between devices  4.55 us (5%)
  other arithmetic  1.48 us (1%)
    pallas_call x1, Pallas kernels, near_attend(): pl.pallas_call(near_kernel, out_shape=tuple((shape(*o) for o in outs)), i...  29.6 us
    pallas_call x1, Pallas kernels, disk_attend(): pl.pallas_call(functools.partial(disk_kernel, pieces=len(pieces)), out_sh...  27.6 us
    ppermute x9, starting transfers between devices, spread(): got.append(lax.ppermute(block, AXES, ring((first, by), (second, by))))  15.7 us
    pallas_call x1, Pallas kernels, prep(): pl.pallas_call(prep_kernel, out_shape=tuple((shape(*o) for o in outs)), i...  8.44 us
    all_to_all x1, starting transfers between devices, local(): lax.all_to_all(send.reshape(devices, 8, width), AXES, split_axis=0, conca...  7.78 us
    ppermute x9, waiting for transfers between devices, spread(): got.append(lax.ppermute(block, AXES, ring((first, by), (second, by))))  4.53 us
    ppermute x4, starting transfers between devices, gather_tokens(): swapped.append(lax.ppermute(piece, AXES, other_core()))  2.81 us
    pallas_call x1, Pallas kernels, place(): pl.pallas_call(place_kernel, out_shape=shape((slots, rows.shape[1]), BF16...  2.65 us
  transfers between devices with their start and end apart: 14, of which 3 were waited for; matrix products, arithmetic and copies ran while one was open for 1% of the time, Pallas kernels for 40%

profile of v6, /device:TPU:0, one launch (start us, length us, event | category | flops | bytes accessed | tf_op | source)
XLA Modules:
  0.0 100.8 jit_solution(10801538887432965)
XLA Ops:
  0.0 4.0 %collective-permute-start.2 = (bf16[5,8,256]{2,1,0:T(8,128)(2,1)}, bf16[5,8,256]{2,1,0:T(8,128)(2,1)S(1)}, u32[]{:S(2)}, u32[]{:S(2)}) collective-permute-start(bf16[5,8,256]{2,1,0:T(8,128)(2,1)} %bitcast.8), channel_id=1, source_target_pairs={{0,64},{1,17},{2,66},{3,19},{4,68},{5,21},{6,70},{7,23},{8,72},{9,... | collective-permute-start | bytes 61448 | tf_op jit(solution)/shard_map/ppermute | solution.py:519
  4.0 0.7 collective-permute-start.1
  4.7 1.3 %collective-permute-start = (bf16[5,8,256]{2,1,0:T(8,128)(2,1)}, bf16[5,8,256]{2,1,0:T(8,128)(2,1)S(1)}, u32[]{:S(2)}, u32[]{:S(2)}) collective-permute-start(bf16[5,8,256]{2,1,0:T(8,128)(2,1)} %bitcast.10), channel_id=1, source_target_pairs={{0,32},{1,9},{2,34},{3,11},{4,36},{5,13},{6,38},{7,15},{8,40},{9,1... | collective-permute-start | bytes 61448 | tf_op jit(solution)/shard_map/ppermute | solution.py:519
  6.0 0.0 collective-permute-done.2
  6.0 2.0 %collective-permute-done.1 = bf16[5,8,256]{2,1,0:T(8,128)(2,1)S(1)} collective-permute-done((bf16[5,8,256]{2,1,0:T(8,128)(2,1)}, bf16[5,8,256]{2,1,0:T(8,128)(2,1)S(1)}, u32[]{:S(2)}, u32[]{:S(2)}) %collective-permute-start.1) | collective-permute-done | bytes 20512 | tf_op jit(solution)/shard_map/ppermute | solution.py:519
  8.0 1.9 %collective-permute-done = bf16[5,8,256]{2,1,0:T(8,128)(2,1)S(1)} collective-permute-done((bf16[5,8,256]{2,1,0:T(8,128)(2,1)}, bf16[5,8,256]{2,1,0:T(8,128)(2,1)S(1)}, u32[]{:S(2)}, u32[]{:S(2)}) %collective-permute-start) | collective-permute-done | bytes 20512 | tf_op jit(solution)/shard_map/ppermute | solution.py:519
  9.9 0.7 pad_maximum_fusion.1
  10.6 3.2 %collective-permute-start.5 = (bf16[5,32,256]{2,1,0:T(8,128)(2,1)S(1)}, bf16[5,32,256]{2,1,0:T(8,128)(2,1)S(1)}, u32[]{:S(2)}, u32[]{:S(2)}) collective-permute-start(bf16[5,32,256]{2,1,0:T(8,128)(2,1)S(1)} %pad_maximum_fusion.1), channel_id=1, source_target_pairs={{0,16},{1,5},{2,18},{3,7},{4,20},{5,1},{6,22},{7,3},{8,24},{9,13},... | collective-permute-start | bytes 245768 | tf_op jit(solution)/shard_map/ppermute | solution.py:519
  13.8 1.1 %collective-permute-start.4 = (bf16[5,32,256]{2,1,0:T(8,128)(2,1)S(1)}, bf16[5,32,256]{2,1,0:T(8,128)(2,1)S(1)}, u32[]{:S(2)}, u32[]{:S(2)}) collective-permute-start(bf16[5,32,256]{2,1,0:T(8,128)(2,1)S(1)} %pad_maximum_fusion.1), channel_id=1, source_target_pairs={{0,24},{1,7},{2,26},{3,1},{4,28},{5,3},{6,30},{7,5},{8,0},{9,15},{... | collective-permute-start | bytes 245768 | tf_op jit(solution)/shard_map/ppermute | solution.py:519
  14.9 1.0 collective-permute-start.3
  15.9 2.6 %place.1 = bf16[1024,256]{1,0:T(8,128)(2,1)} custom-call(s32[1,512]{1,0:T(1,128)} %bitcast.14, bf16[512,256]{1,0:T(8,128)(2,1)} %rows_ref.1), custom_call_target="tpu_custom_call" | custom-call | flops 1000000000 | bytes 1000000 | tf_op jit(solution)/shard_map/place/pallas_call | solution.py:71
  18.5 7.8 %all-to-all-start = ((bf16[128,8,256]{2,1,0:T(8,128)(2,1)}), bf16[128,8,256]{2,1,0:T(8,128)(2,1)}, u32[]{:S(2)}, u32[]{:S(2)}) async-start(bf16[128,8,256]{2,1,0:T(8,128)(2,1)} %bitcast.7), calls=%async_computation | async-start | bytes 1048576 | tf_op jit(solution)/shard_map/all_to_all | solution.py:556
  26.3 0.7 pad_maximum_fusion.refs_3_
  27.1 0.9 collective-permute-start.8
  28.0 2.4 %collective-permute-start.7 = (bf16[5,128,256]{2,1,0:T(8,128)(2,1)}, bf16[5,128,256]{2,1,0:T(8,128)(2,1)}, u32[]{:S(2)}, u32[]{:S(2)}) collective-permute-start(bf16[5,128,256]{2,1,0:T(8,128)(2,1)} %pad_maximum_fusion.refs_3_), channel_id=1, source_target_pairs={{0,6},{1,97},{2,0},{3,99},{4,2},{5,101},{6,4},{7,103},{8,14},{9,10... | collective-permute-start | bytes 983048 | tf_op jit(solution)/shard_map/ppermute | solution.py:519
  30.3 1.2 %collective-permute-start.6 = (bf16[5,128,256]{2,1,0:T(8,128)(2,1)}, bf16[5,128,256]{2,1,0:T(8,128)(2,1)}, u32[]{:S(2)}, u32[]{:S(2)}) collective-permute-start(bf16[5,128,256]{2,1,0:T(8,128)(2,1)} %pad_maximum_fusion.refs_3_), channel_id=1, source_target_pairs={{0,4},{1,65},{2,6},{3,67},{4,0},{5,69},{6,2},{7,71},{8,12},{9,73},... | collective-permute-start | bytes 983048 | tf_op jit(solution)/shard_map/ppermute | solution.py:519
  31.5 8.4 %prep.1 = (bf16[8192,256]{1,0:T(8,128)(2,1)}, f32[512,128]{1,0:T(8,128)}) custom-call(s32[32,512]{1,0:T(8,128)} %bitcast.12, s32[32,512]{1,0:T(8,128)} %bitcast.13, bf16[512,512]{1,0:T(8,128)(2,1)} %refs_17_.1, f32[1,512]{1,0:T(1,128)} %bitcast.15, bf16[512,512]{1,0:T(8,128)(2,1)} %wq_hbm.1, bf16[512,1024]{1,0:T(8,128)(2,1)} %wkv_hbm.1, ...), custom_call_target="tpu_custom_call" | custom-call | flops 8000000000 | bytes 8000000 | tf_op jit(solution)/shard_map/prep/pallas_call | solution.py:161
  40.0 0.1 collective-permute-start.9
  40.1 0.5 collective-permute-start.12
  40.6 0.1 collective-permute-start.11
  40.7 0.6 collective-permute-done.6.refs_4_
  41.3 2.1 %collective-permute-start.10 = (bf16[5,128,256]{2,1,0:T(8,128)(2,1)}, bf16[5,128,256]{2,1,0:T(8,128)(2,1)}, u32[]{:S(2)}, u32[]{:S(2)}) collective-permute-start(bf16[5,128,256]{2,1,0:T(8,128)(2,1)} %collective-permute-done.6.refs_4_), channel_id=1, source_target_pairs={{0,1},{1,0},{2,3},{3,2},{4,5},{5,4},{6,7},{7,6},{8,9},{9,8},{10,11... | collective-permute-start | bytes 983048 | tf_op jit(solution)/shard_map/ppermute | solution.py:532
  43.4 29.6 %near_attend.1 = (f32[512,128]{1,0:T(8,128)}, f32[512,128]{1,0:T(8,128)}, f32[512,512]{1,0:T(8,128)}) custom-call(bf16[1024,256]{1,0:T(8,128)(2,1)} %bitcast.6.got_hbm, bf16[256,1024]{1,0:T(8,128)(2,1)} %w_hbm.1, bf16[8192,256]{1,0:T(8,128)(2,1)} %get-tuple-element.10.all_hbm.refs_2_, f32[512,128]{1,0:T(8,128)} %get-tuple-element.11.own_hbm.refs_11_), custom_call_target="tpu_custom_call" | custom-call | flops 5000000000 | bytes 5000000 | tf_op jit(solution)/shard_map/near_attend/pallas_call | solution.py:292
  73.1 27.6 %disk_attend.1 = bf16[512,512]{1,0:T(8,128)(2,1)} custom-call(s32[5]{0:T(128)} %refs_0_.1, s32[5]{0:T(128)} %refs_1_.1, bf16[8192,256]{1,0:T(8,128)(2,1)} %get-tuple-element.10.all_hbm.refs_2_, bf16[5,128,256]{2,1,0:T(8,128)(2,1)} %pad_maximum_fusion.refs_3_, bf16[5,128,256]{2,1,0:T(8,128)(2,1)} %collective-permute-done.6.refs_4_, ...), custom_call_target="tpu_custom_call" | custom-call | flops 16000000000 | bytes 10000000 | tf_op jit(solution)/shard_map/disk_attend/pallas_call | solution.py:470
  (10 shorter events, 0.0 us)
Async XLA Ops:
  0.0 6.0 %collective-permute-start.2 = (bf16[5,8,256]{2,1,0:T(8,128)(2,1)}, bf16[5,8,256]{2,1,0:T(8,128)(2,1)S(1)}, u32[]{:S(2)}, u32[]{:S(2)}) collective-permute-start(bf16[5,8,256]{2,1,0:T(8,128)(2,1)} %bitcast.8), channel_id=1, source_target_pairs={{0,64},{1,17},{2,66},{3,19},{4,68},{5,21},{6,70},{7,23},{8,72},{9,... | collective-permute-start | bytes 61448 | tf_op jit(solution)/shard_map/ppermute | solution.py:519
  4.0 4.0 %collective-permute-start.1 = (bf16[5,8,256]{2,1,0:T(8,128)(2,1)}, bf16[5,8,256]{2,1,0:T(8,128)(2,1)S(1)}, u32[]{:S(2)}, u32[]{:S(2)}) collective-permute-start(bf16[5,8,256]{2,1,0:T(8,128)(2,1)} %bitcast.9), channel_id=1, source_target_pairs={{0,96},{1,25},{2,98},{3,27},{4,100},{5,29},{6,102},{7,31},{8,104},... | collective-permute-start | bytes 61448 | tf_op jit(solution)/shard_map/ppermute | solution.py:519
  4.7 5.2 %collective-permute-start = (bf16[5,8,256]{2,1,0:T(8,128)(2,1)}, bf16[5,8,256]{2,1,0:T(8,128)(2,1)S(1)}, u32[]{:S(2)}, u32[]{:S(2)}) collective-permute-start(bf16[5,8,256]{2,1,0:T(8,128)(2,1)} %bitcast.10), channel_id=1, source_target_pairs={{0,32},{1,9},{2,34},{3,11},{4,36},{5,13},{6,38},{7,15},{8,40},{9,1... | collective-permute-start | bytes 61448 | tf_op jit(solution)/shard_map/ppermute | solution.py:519
  10.6 15.7 %collective-permute-start.5 = (bf16[5,32,256]{2,1,0:T(8,128)(2,1)S(1)}, bf16[5,32,256]{2,1,0:T(8,128)(2,1)S(1)}, u32[]{:S(2)}, u32[]{:S(2)}) collective-permute-start(bf16[5,32,256]{2,1,0:T(8,128)(2,1)S(1)} %pad_maximum_fusion.1), channel_id=1, source_target_pairs={{0,16},{1,5},{2,18},{3,7},{4,20},{5,1},{6,22},{7,3},{8,24},{9,13},... | collective-permute-start | bytes 245768 | tf_op jit(solution)/shard_map/ppermute | solution.py:519
  13.8 12.5 %collective-permute-start.4 = (bf16[5,32,256]{2,1,0:T(8,128)(2,1)S(1)}, bf16[5,32,256]{2,1,0:T(8,128)(2,1)S(1)}, u32[]{:S(2)}, u32[]{:S(2)}) collective-permute-start(bf16[5,32,256]{2,1,0:T(8,128)(2,1)S(1)} %pad_maximum_fusion.1), channel_id=1, source_target_pairs={{0,24},{1,7},{2,26},{3,1},{4,28},{5,3},{6,30},{7,5},{8,0},{9,15},{... | collective-permute-start | bytes 245768 | tf_op jit(solution)/shard_map/ppermute | solution.py:519
  14.9 11.4 %collective-permute-start.3 = (bf16[5,32,256]{2,1,0:T(8,128)(2,1)S(1)}, bf16[5,32,256]{2,1,0:T(8,128)(2,1)S(1)}, u32[]{:S(2)}, u32[]{:S(2)}) collective-permute-start(bf16[5,32,256]{2,1,0:T(8,128)(2,1)S(1)} %pad_maximum_fusion.1), channel_id=1, source_target_pairs={{0,8},{1,3},{2,10},{3,5},{4,12},{5,7},{6,14},{7,1},{8,16},{9,11},{... | collective-permute-start | bytes 245768 | tf_op jit(solution)/shard_map/ppermute | solution.py:519
  18.5 24.9 %all-to-all-start = ((bf16[128,8,256]{2,1,0:T(8,128)(2,1)}), bf16[128,8,256]{2,1,0:T(8,128)(2,1)}, u32[]{:S(2)}, u32[]{:S(2)}) async-start(bf16[128,8,256]{2,1,0:T(8,128)(2,1)} %bitcast.7), calls=%async_computation | async-start | bytes 1048576 | tf_op jit(solution)/shard_map/all_to_all | solution.py:556
  27.1 13.0 %collective-permute-start.8 = (bf16[5,128,256]{2,1,0:T(8,128)(2,1)}, bf16[5,128,256]{2,1,0:T(8,128)(2,1)}, u32[]{:S(2)}, u32[]{:S(2)}) collective-permute-start(bf16[5,128,256]{2,1,0:T(8,128)(2,1)} %pad_maximum_fusion.refs_3_), channel_id=1, source_target_pairs={{0,2},{1,33},{2,4},{3,35},{4,6},{5,37},{6,0},{7,39},{8,10},{9,41},... | collective-permute-start | bytes 983048 | tf_op jit(solution)/shard_map/ppermute | solution.py:519
  28.0 12.6 %collective-permute-start.7 = (bf16[5,128,256]{2,1,0:T(8,128)(2,1)}, bf16[5,128,256]{2,1,0:T(8,128)(2,1)}, u32[]{:S(2)}, u32[]{:S(2)}) collective-permute-start(bf16[5,128,256]{2,1,0:T(8,128)(2,1)} %pad_maximum_fusion.refs_3_), channel_id=1, source_target_pairs={{0,6},{1,97},{2,0},{3,99},{4,2},{5,101},{6,4},{7,103},{8,14},{9,10... | collective-permute-start | bytes 983048 | tf_op jit(solution)/shard_map/ppermute | solution.py:519
  30.3 11.0 %collective-permute-start.6 = (bf16[5,128,256]{2,1,0:T(8,128)(2,1)}, bf16[5,128,256]{2,1,0:T(8,128)(2,1)}, u32[]{:S(2)}, u32[]{:S(2)}) collective-permute-start(bf16[5,128,256]{2,1,0:T(8,128)(2,1)} %pad_maximum_fusion.refs_3_), channel_id=1, source_target_pairs={{0,4},{1,65},{2,6},{3,67},{4,0},{5,69},{6,2},{7,71},{8,12},{9,73},... | collective-permute-start | bytes 983048 | tf_op jit(solution)/shard_map/ppermute | solution.py:519
  40.0 33.1 %collective-permute-start.9 = (bf16[5,128,256]{2,1,0:T(8,128)(2,1)}, bf16[5,128,256]{2,1,0:T(8,128)(2,1)}, u32[]{:S(2)}, u32[]{:S(2)}) collective-permute-start(bf16[5,128,256]{2,1,0:T(8,128)(2,1)} %pad_maximum_fusion.refs_3_), channel_id=1, source_target_pairs={{0,1},{1,0},{2,3},{3,2},{4,5},{5,4},{6,7},{7,6},{8,9},{9,8},{10,11... | collective-permute-start | bytes 983048 | tf_op jit(solution)/shard_map/ppermute | solution.py:532
  40.1 33.0 %collective-permute-start.12 = (bf16[5,128,256]{2,1,0:T(8,128)(2,1)}, bf16[5,128,256]{2,1,0:T(8,128)(2,1)}, u32[]{:S(2)}, u32[]{:S(2)}) collective-permute-start(bf16[5,128,256]{2,1,0:T(8,128)(2,1)} %collective-permute-done.8.refs_6_), channel_id=1, source_target_pairs={{0,1},{1,0},{2,3},{3,2},{4,5},{5,4},{6,7},{7,6},{8,9},{9,8},{10,11... | collective-permute-start | bytes 983048 | tf_op jit(solution)/shard_map/ppermute | solution.py:532
  40.6 32.5 %collective-permute-start.11 = (bf16[5,128,256]{2,1,0:T(8,128)(2,1)}, bf16[5,128,256]{2,1,0:T(8,128)(2,1)}, u32[]{:S(2)}, u32[]{:S(2)}) collective-permute-start(bf16[5,128,256]{2,1,0:T(8,128)(2,1)} %collective-permute-done.7.refs_5_), channel_id=1, source_target_pairs={{0,1},{1,0},{2,3},{3,2},{4,5},{5,4},{6,7},{7,6},{8,9},{9,8},{10,11... | collective-permute-start | bytes 983048 | tf_op jit(solution)/shard_map/ppermute | solution.py:532
  41.3 31.8 %collective-permute-start.10 = (bf16[5,128,256]{2,1,0:T(8,128)(2,1)}, bf16[5,128,256]{2,1,0:T(8,128)(2,1)}, u32[]{:S(2)}, u32[]{:S(2)}) collective-permute-start(bf16[5,128,256]{2,1,0:T(8,128)(2,1)} %collective-permute-done.6.refs_4_), channel_id=1, source_target_pairs={{0,1},{1,0},{2,3},{3,2},{4,5},{5,4},{6,7},{7,6},{8,9},{9,8},{10,11... | collective-permute-start | bytes 983048 | tf_op jit(solution)/shard_map/ppermute | solution.py:532
